TPU v7x, 32 devices: a whole 2x2x4 slice. The times are simulated.
32 devices in a mesh: dp: 4 (over z), expert: 8 (over y, x, core).
Axes of the slice: x: 2, y: 2, z: 4, core: 2. Of those that a mesh axis runs over, the one named last changes fastest.
Arguments:
- tokens: bfloat16 [8192, 1536], P(('dp', 'expert')), may hold values from -6 to 6
- segment_ids: int32 [8192], P('dp'), may hold values from 0 to 7, never falling along the last dimension, each value on 1 to 2048 neighbouring positions
- expert_ids: int32 [8192, 8], P(('dp', 'expert')), may hold values from 0 to 15, all different within a row; in each aligned block of 256 rows (0 to 255, 256 to 511, ...) at most 160 rows name the same one
- w_query: bfloat16 [1536, 1536], P(('dp', 'expert')), may hold values from -0.5 to 0.5
- w_key_value: bfloat16 [1536, 1024], P(('dp', 'expert')), may hold values from -0.5 to 0.5
- w_out: bfloat16 [1536, 1536], P(None, ('dp', 'expert')), may hold values from -1.75 to 1.75
- w_router: bfloat16 [1536, 16], P(('dp', 'expert')), may hold values from -0.078125 to 0.078125
- norm_attn: bfloat16 [1536], P(('dp', 'expert')), may hold values from 0.5 to 1.5
- norm_moe: bfloat16 [1536], P(('dp', 'expert')), may hold values from 0.5 to 1.5
- w_gate_up: bfloat16 [16, 1536, 1024], P('expert'), may hold values from -0.15625 to 0.15625
- w_down: bfloat16 [16, 512, 1536], P('expert'), may hold values from -6 to 6
- grad_out: bfloat16 [8192, 1536], P(('dp', 'expert')), may hold values from -6 to 6
Outputs:
- result: bfloat16 [8192, 1536], P(('dp', 'expert'))
- grad_tokens: bfloat16 [8192, 1536], P(('dp', 'expert'))
- grad_w_query: float32 [1536, 1536], P(('dp', 'expert'))
- grad_w_key_value: float32 [1536, 1024], P(('dp', 'expert'))
- grad_w_out: float32 [1536, 1536], P(None, ('dp', 'expert'))
- grad_w_router: float32 [1536, 16], P(('dp', 'expert'))
- grad_norm_attn: float32 [1536], P(('dp', 'expert'))
- grad_norm_moe: float32 [1536], P(('dp', 'expert'))
- grad_w_gate_up: float32 [16, 1536, 1024], P('expert', 'dp')
- grad_w_down: float32 [16, 512, 1536], P('expert', None, 'dp')
Inputs may be any that keep to these rules, and one draw needn't show every extreme that they name: `expert_ids`: within the 256 tokens of one device a row names 8 different experts, and no expert is named more than 160 times; in every draw some expert is named exactly 160 times by one device's tokens.
All inputs are finite; a program needn't handle non-finite values.
Results may differ from a plain program's by a relative error of at most 0.02.
Values may be sent and summed in bfloat16 or wider, within the bound.
No kernel may reach another device: no remote copies, remote signals or barrier semaphores. Data moves between devices by JAX's collectives and lax.ppermute only.
A program may use at most 256 MiB of HBM per device.

v0:
```python
import functools

import jax
import jax.numpy as jnp
from jax import lax
from jax.experimental import pallas as pl
from jax.experimental.pallas import tpu as pltpu
from jax.sharding import PartitionSpec as P

D = 1536
HEADS = 24
KV_HEADS = 8
HEAD_DIM = 64
FF = 512
TOP = 8
EXP_DEV = 2

RESIDUAL = 0.22
ATTN_SCALE = 0.015625
LOG2E = 1.4426950408889634
EPSILON = 1e-06
ROPE_BASE = 10000.0
MASKED = -1e30

GROUP = HEADS // KV_HEADS
HALF = HEAD_DIM // 2
BLK = 256
BF = jnp.bfloat16
F32 = jnp.float32
BOTH = ("dp", "expert")


def cost(micros):
    return pl.CostEstimate(flops=micros * 10**9, bytes_accessed=10**4, transcendentals=0)


LONG, SHORT = cost(50), cost(0)


def dot(a, b, ca, cb):
    return lax.dot_general(a, b, (((ca,), (cb,)), ((), ())), preferred_element_type=F32)


def rms_scale(values, gain_vec):
    return (
        values * lax.rsqrt(jnp.mean(values * values, axis=-1, keepdims=True) + EPSILON) * gain_vec
    )


def side_by_side(block):
    return jnp.concatenate(
        [block[h * HEAD_DIM : (h + 1) * HEAD_DIM] for h in range(GROUP)], axis=1
    )


def stacked(wide):
    width = wide.shape[1] // GROUP
    return jnp.concatenate([wide[:, h * width : (h + 1) * width] for h in range(GROUP)], axis=0)


def allowed_keys(start_ref, block, key_block):
    lane = lax.broadcasted_iota(jnp.int32, (1, BLK), 1) + block * BLK
    reach = lane - start_ref[...]
    lane3 = jnp.concatenate([lane] * GROUP, axis=1)
    reach3 = jnp.concatenate([reach] * GROUP, axis=1)
    key_pos = lax.broadcasted_iota(jnp.int32, (BLK, 1), 0) + key_block * BLK
    back = lane3 - key_pos
    return (back >= 0) & (back <= reach3)


def over_keys(first_ref, block, step, carry):
    clear = jnp.minimum(first_ref[1, block], block)
    carry = lax.fori_loop(first_ref[0, block], clear, functools.partial(step, True), carry)
    pairs = (block - clear) // 2
    carry = lax.fori_loop(
        0, pairs, lambda n, carry: step(False, clear + 2 * n, carry, 2), carry
    )
    carry = lax.fori_loop(clear + 2 * pairs, block, functools.partial(step, False), carry)
    return step(True, block, carry)


def attn_fwd_kernel(first_ref, q_ref, k_ref, vt_ref, start_ref, a_ref, o_ref, lse_ref):
    block = pl.program_id(0)
    query = side_by_side(q_ref[...])
    width = GROUP * BLK

    def step(masked, key_block, carry, count=1):
        largest, total, acc = carry
        rows = pl.ds(pl.multiple_of(key_block * BLK, BLK), count * BLK)
        keys, values = k_ref[rows, :], vt_ref[:, rows]
        scores = dot(keys, query, 1, 0) * (ATTN_SCALE * LOG2E)
        if masked:
            scores = jnp.where(allowed_keys(start_ref, block, key_block), scores, MASKED)
        now = jnp.maximum(largest, jnp.max(scores, axis=0, keepdims=True))
        power = jnp.exp2(scores - now)
        fade = jnp.exp2(largest - now)
        total = total * fade + jnp.sum(power, axis=0, keepdims=True)
        acc = acc * fade + dot(values, power.astype(BF), 1, 0)
        return now, total, acc

    largest, total, acc = over_keys(
        first_ref,
        block,
        step,
        (
            jnp.full((1, width), MASKED, F32),
            jnp.zeros((1, width), F32),
            jnp.zeros((HEAD_DIM, width), F32),
        ),
    )
    out = stacked(acc / total)
    o_ref[...] = out
    a_ref[...] = out.astype(BF)
    lse = largest + jnp.log2(total)
    lse_ref[...] = jnp.concatenate(
        [lse[:, h * BLK : (h + 1) * BLK] for h in range(GROUP)]
        + [jnp.zeros((8 - GROUP, BLK), F32)],
        axis=0,
    )


def attn_bwd_kernel(
    first_ref, q_ref, da_ref, o_ref, lse_ref, k_ref, kt_ref, v_ref, start_ref,
    dq_ref, dk_ref, dv_ref, dk_acc, dv_acc,
):
    block = pl.program_id(0)

    @pl.when(block == 0)
    def _():
        dk_acc[...] = jnp.zeros_like(dk_acc)
        dv_acc[...] = jnp.zeros_like(dv_acc)

    query_t = side_by_side(q_ref[...])
    query = query_t.astype(F32).T.astype(BF)
    grad_t = side_by_side(da_ref[0])
    grad_f = grad_t.astype(F32)
    grad = grad_f.T.astype(BF)
    delta = jnp.sum(side_by_side(o_ref[...]) * grad_f, axis=0, keepdims=True)
    lse = jnp.concatenate([lse_ref[h : h + 1, :] for h in range(GROUP)], axis=1)

    def step(masked, key_block, dq, count=1):
        rows = pl.ds(pl.multiple_of(key_block * BLK, BLK), count * BLK)
        keys = k_ref[rows, :]
        scores = dot(keys, query_t, 1, 0) * (ATTN_SCALE * LOG2E)
        if masked:
            scores = jnp.where(allowed_keys(start_ref, block, key_block), scores, MASKED)
        prob = jnp.exp2(scores - lse)
        grad_prob = dot(v_ref[rows, :], grad_t, 1, 0)
        grad_score = (prob * (grad_prob - delta) * ATTN_SCALE).astype(BF)
        dv_acc[rows, :] += dot(prob.astype(BF), grad, 1, 0)
        dk_acc[rows, :] += dot(grad_score, query, 1, 0)
        return dq + dot(kt_ref[:, rows], grad_score, 1, 0)

    dq = over_keys(first_ref, block, step, jnp.zeros((HEAD_DIM, GROUP * BLK), F32))
    dq_ref[...] = stacked(dq)

    @pl.when(block == pl.num_programs(0) - 1)
    def _():
        dk_ref[...] = dk_acc[...].T
        dv_ref[...] = dv_acc[...].T


def attn_forward(first, q_t, k, v_t, start):
    seq = q_t.shape[1]
    rows = GROUP * HEAD_DIM
    column = lambda g, first: (0, g)
    whole = lambda g, first: (0, 0)
    return pl.pallas_call(
        attn_fwd_kernel,
        grid_spec=pltpu.PrefetchScalarGridSpec(
            num_scalar_prefetch=1,
            grid=(seq // BLK,),
            in_specs=[
                pl.BlockSpec((rows, BLK), column),
                pl.BlockSpec((seq, HEAD_DIM), whole),
                pl.BlockSpec((HEAD_DIM, seq), whole),
                pl.BlockSpec((1, BLK), column),
            ],
            out_specs=[
                pl.BlockSpec((rows, BLK), column),
                pl.BlockSpec((rows, BLK), column),
                pl.BlockSpec((8, BLK), column),
            ],
        ),
        out_shape=[
            jax.ShapeDtypeStruct((rows, seq), BF),
            jax.ShapeDtypeStruct((rows, seq), F32),
            jax.ShapeDtypeStruct((8, seq), F32),
        ],
        cost_estimate=LONG,
        name="attn_fwd",
    )(first, q_t, k, v_t, start)


def attn_backward(first, q_t, da, o_t, lse, k, k_t, v, start):
    seq = q_t.shape[1]
    rows = GROUP * HEAD_DIM
    column = lambda g, first: (0, g)
    whole = lambda g, first: (0, 0)
    return pl.pallas_call(
        attn_bwd_kernel,
        grid_spec=pltpu.PrefetchScalarGridSpec(
            num_scalar_prefetch=1,
            grid=(seq // BLK,),
            in_specs=[
                pl.BlockSpec((rows, BLK), column),
                pl.BlockSpec((1, rows, BLK), lambda g, first: (g, 0, 0)),
                pl.BlockSpec((rows, BLK), column),
                pl.BlockSpec((8, BLK), column),
                pl.BlockSpec((seq, HEAD_DIM), whole),
                pl.BlockSpec((HEAD_DIM, seq), whole),
                pl.BlockSpec((seq, HEAD_DIM), whole),
                pl.BlockSpec((1, BLK), column),
            ],
            out_specs=[
                pl.BlockSpec((rows, BLK), column),
                pl.BlockSpec((HEAD_DIM, seq), whole),
                pl.BlockSpec((HEAD_DIM, seq), whole),
            ],
            scratch_shapes=[
                pltpu.VMEM((seq, HEAD_DIM), F32),
                pltpu.VMEM((seq, HEAD_DIM), F32),
            ],
        ),
        out_shape=[
            jax.ShapeDtypeStruct((rows, seq), F32),
            jax.ShapeDtypeStruct((HEAD_DIM, seq), F32),
            jax.ShapeDtypeStruct((HEAD_DIM, seq), F32),
        ],
        cost_estimate=cost(20),
        name="attn_bwd",
    )(first, q_t, da, o_t, lse, k, k_t, v, start)


PACK = 384
Q_COLS = GROUP * HEAD_DIM
QKV = Q_COLS + 2 * HEAD_DIM
ROUTE = QKV - 256


def spec(shape, index):
    return pl.BlockSpec(shape, index)


def resident(shape):
    return pl.BlockSpec(
        shape, lambda *_: (0,) * len(shape), pipeline_mode=pl.Buffered(1)
    )


def call(kernel, name, grid, in_specs, out_specs, out_shape, estimate, scratch=()):
    return pl.pallas_call(
        kernel,
        grid_spec=pltpu.PrefetchScalarGridSpec(
            num_scalar_prefetch=1,
            grid=grid,
            in_specs=in_specs,
            out_specs=out_specs,
            scratch_shapes=list(scratch),
        ),
        out_shape=out_shape,
        cost_estimate=estimate,
        name=name,
    )


def shape(dims, kind):
    return jax.ShapeDtypeStruct(dims, kind)


PAIR = 2 * BLK


def far_pair(step, pos):
    return step ^ (pos[0] // 2)


def halves(pos):
    core = pos[0] % 2
    return [pl.ds(pl.multiple_of(start * BLK, BLK), BLK) for start in (1 - core, core)]


def turn_rows(rows_t, cosine, sine):
    out = []
    for h in range(rows_t.shape[0] // HEAD_DIM):
        a = rows_t[h * HEAD_DIM : h * HEAD_DIM + HALF]
        b = rows_t[h * HEAD_DIM + HALF : (h + 1) * HEAD_DIM]
        out += [a * cosine - b * sine, b * cosine + a * sine]
    return jnp.concatenate(out, axis=0)


def norm_of(values):
    return values * lax.rsqrt(jnp.mean(values * values, axis=1, keepdims=True) + EPSILON)


def qkv_kernel(count, pos_ref, *refs):
    pieces = refs[: count + 2]
    w_ref, gain_ref, cos_ref, sin_ref, q_ref, kt_ref, vt_ref, k_ref, v_ref = refs[count + 2 :]
    gain = gain_ref[...]
    for r in range(count):
        if r < count - 2:
            rows = pieces[r][...]
        else:
            at = count - 2 + 2 * (r - count + 2)
            rows = jnp.concatenate([pieces[at][...], pieces[at + 1][...]], axis=0)
        normed = (norm_of(rows.astype(F32)) * gain).astype(BF)
        both = dot(normed, w_ref[...], 1, 0)
        turned = both.T
        place = pl.multiple_of((pos_ref[0] ^ r) * BLK, BLK)
        columns = pl.ds(place, BLK)
        cosine, sine = cos_ref[:, columns], sin_ref[:, columns]
        qk = turn_rows(turned[: Q_COLS + HEAD_DIM], cosine, sine)
        q_ref[:, columns] = qk[:Q_COLS].astype(BF)
        kt_ref[:, columns] = qk[Q_COLS:].astype(BF)
        vt_ref[:, columns] = turned[Q_COLS + HEAD_DIM : QKV].astype(BF)
        k_ref[columns, :] = qk[Q_COLS:].T.astype(BF)
        v_ref[columns, :] = both[:, 256 : 256 + HEAD_DIM].astype(BF)


def qkv_forward(pos, pieces, weights, gain, cosine, sine):
    count = len(pieces) - 2
    seq = cosine.shape[1]
    full = lambda a: resident(a.shape)
    return call(
        functools.partial(qkv_kernel, count),
        "qkv",
        (1,),
        [full(a) for a in pieces] + [full(a) for a in (weights, gain, cosine, sine)],
        [resident(s) for s in ((Q_COLS, seq), (HEAD_DIM, seq), (HEAD_DIM, seq), (seq, HEAD_DIM), (seq, HEAD_DIM))],
        [
            shape((Q_COLS, seq), BF),
            shape((HEAD_DIM, seq), BF),
            shape((HEAD_DIM, seq), BF),
            shape((seq, HEAD_DIM), BF),
            shape((seq, HEAD_DIM), BF),
        ],
        cost(400),
    )(pos, *pieces, weights, gain, cosine, sine)


def send_weights_kernel(groups, members, pos_ref, q_ref, kv_ref, rest_ref, out_ref):
    query, pair, rest = q_ref[...], kv_ref[...], rest_ref[...]
    for j in range(members):
        block = jnp.concatenate(
            [query[:, j * Q_COLS : (j + 1) * Q_COLS]]
            + [pair[:, n * HEAD_DIM : (n + 1) * HEAD_DIM] for n in (j, members + j)]
            + [rest],
            axis=1,
        )
        for i in range(groups):
            out_ref[i * members + j] = block


def send_weights(pos, w_query, w_key_value, rest, groups, members):
    rows = w_query.shape[0]
    full = lambda a: resident(a.shape)
    return call(
        functools.partial(send_weights_kernel, groups, members),
        "send_weights",
        (1,),
        [full(a) for a in (w_query, w_key_value, rest)],
        resident((groups * members, rows, PACK)),
        shape((groups * members, rows, PACK), BF),
        SHORT,
    )(pos, w_query, w_key_value, rest)


def mix_kernel(count, pos_ref, *refs):
    pieces = refs[: count + 2]
    x_ref, w_ref, gain_ref, route_ref, ids_ref = refs[count + 2 : count + 7]
    h2_ref, gates_ref, y1_ref, h2_own_ref, gates_own_ref, heads, y1_all = refs[count + 7 :]
    block = pl.program_id(0)
    pos = pos_ref[0]
    for r in range(count):
        base = (pos ^ r) * Q_COLS
        if r < count - 2:
            heads[pl.ds(pl.multiple_of(base, Q_COLS), Q_COLS), :] = pieces[r][...]
        else:
            half = Q_COLS // 2
            at = count - 2 + 2 * (r - count + 2)
            heads[pl.ds(pl.multiple_of(base, half), half), :] = pieces[at][...]
            heads[pl.ds(pl.multiple_of(base + half, half), half), :] = pieces[at + 1][...]
    route, gain = route_ref[...], gain_ref[...]
    for h in range(2):
        rows = slice(h * BLK, (h + 1) * BLK)
        mixed = dot(heads[:, rows], w_ref[...], 0, 0)
        y1 = x_ref[h ^ (pos % 2)].astype(F32) + RESIDUAL * mixed
        h2 = (norm_of(y1) * gain).astype(BF)
        logits = dot(h2, route, 1, 0)
        lane = lax.broadcasted_iota(jnp.int32, logits.shape, 1) - ROUTE
        ids = ids_ref[h ^ (pos % 2)].T
        chosen = lane == ids[:, 0:1]
        for k in range(1, TOP):
            chosen = chosen | (lane == ids[:, k : k + 1])
        masked = jnp.where(chosen, logits, MASKED)
        power = jnp.where(chosen, jnp.exp(masked - jnp.max(masked, axis=1, keepdims=True)), 0.0)
        gates = power / jnp.sum(power, axis=1, keepdims=True)
        h2_ref[rows] = h2
        gates_ref[rows] = gates
        y1_all[rows] = y1

    @pl.when(block == pos // 2)
    def _():
        mine = halves(pos_ref)[1]
        y1_ref[...] = y1_all[mine]
        h2_own_ref[...] = h2_ref[mine]
        gates_own_ref[...] = gates_ref[mine]


def mix_forward(pos, pieces, x_rel, w_full, gain, weights, ids):
    count = len(pieces) - 2
    seq = ids.shape[0] * BLK
    row = lambda s, pos: (s, 0)
    return call(
        functools.partial(mix_kernel, count),
        "mix",
        (seq // PAIR,),
        [spec((a.shape[0], PAIR), lambda s, pos: (0, s)) for a in pieces]
        + [
            spec((2, BLK, D), lambda s, pos: (far_pair(s, pos), 0, 0)),
            resident(w_full.shape),
            resident(gain.shape),
            pl.BlockSpec((D, 128), lambda s, pos: (0, 2), pipeline_mode=pl.Buffered(1)),
            spec((2, TOP, BLK), lambda s, pos: (far_pair(s, pos), 0, 0)),
        ],
        [
            spec((PAIR, D), row),
            spec((PAIR, 128), row),
            resident((BLK, D)),
            resident((BLK, D)),
            resident((BLK, 128)),
        ],
        [
            shape((seq, D), BF),
            shape((seq, 128), F32),
            shape((BLK, D), F32),
            shape((BLK, D), BF),
            shape((BLK, 128), F32),
        ],
        LONG,
        [pltpu.VMEM((HEADS * HEAD_DIM, PAIR), BF), pltpu.VMEM((PAIR, D), F32)],
    )(pos, *pieces, x_rel, w_full, gain, weights, ids)


def expert_kernel(e, pos_ref, h2_ref, dy_ref, gates_ref, up_ref, down_ref, *refs):
    if e == 0:
        ag_ref, dgu_ref, sum_ref, dg_ref, grad_ref, grad_acc = refs

        @pl.when(pl.program_id(0) == 0)
        def _():
            grad_acc[...] = jnp.zeros_like(grad_acc)

    else:
        sum_ref, dg_in_ref, ag_ref, dgu_ref, give_ref, keep_ref, dg_ref = refs
    for h, rows in enumerate(halves(pos_ref)):
        h2, dy, gates = h2_ref[rows], dy_ref[rows], gates_ref[rows]
        which = lax.broadcasted_iota(jnp.int32, gates.shape, 1)
        here = which == ROUTE + EXP_DEV * pos_ref[0] + e
        gate = RESIDUAL * jnp.sum(jnp.where(here, gates, 0.0), axis=1, keepdims=True)
        gu = dot(h2, up_ref[0], 1, 0)
        back = dot(dy, down_ref[0], 1, 1)
        g, u = gu[:, :FF], gu[:, FF:]
        sig = 1.0 / (1.0 + jnp.exp(-g))
        swish = g * sig
        act = swish * u
        gate_grad = RESIDUAL * jnp.sum(act * back, axis=1, keepdims=True)
        gate_grad = jnp.where(which == e, gate_grad, 0.0).T[:8]
        ag_ref[rows] = (gate * act).astype(BF)
        dact = gate * back
        dgu = jnp.concatenate(
            [dact * u * (sig * (1.0 + g * (1.0 - sig))), dact * swish], axis=1
        ).astype(BF)
        dgu_ref[rows] = dgu
        total = dot(dgu, up_ref[0], 1, 1)
        place = pos_ref[0] % 2 if h else 1 - pos_ref[0] % 2
        if e == 0:
            sum_ref[rows] = total
            dg_ref[place] = gate_grad
        else:
            (keep_ref if h else give_ref)[0] = (sum_ref[rows] + total).astype(BF)
            dg_ref[place] = dg_in_ref[place] + gate_grad
    if e == 0:
        grad_acc[...] += dot(ag_ref[...], dy_ref[...], 0, 0)

        @pl.when(pl.program_id(0) == pl.num_programs(0) - 1)
        def _():
            put_shares(grad_ref, grad_acc)


def expert_pass(e, pos, h2, dy_all, gates, w_gate_up, w_down, carried=()):
    seq = h2.shape[0]
    row = lambda s, pos: (s, 0)
    blocks = lambda s, pos: (s, 0, 0)
    pair = lambda s, pos: (far_pair(s, pos), 0, 0)
    half = seq // PAIR
    one = lambda a: pl.BlockSpec(
        (1,) + a.shape[1:], lambda s, pos: (e, 0, 0), pipeline_mode=pl.Buffered(1)
    )
    sums = (spec((PAIR, D), row), shape((seq, D), F32))
    gate_grads = (spec((2, 8, BLK), blocks), shape((2 * half, 8, BLK), F32))
    outs = [
        (spec((PAIR, FF), row), shape((seq, FF), BF)),
        (spec((PAIR, 2 * FF), row), shape((seq, 2 * FF), BF)),
    ]
    if e == 0:
        shares = (D // SHARE, FF, SHARE)
        outs += [sums, gate_grads, (resident(shares), shape(shares, BF))]
    else:
        outs += 2 * [(spec((1, BLK, D), pair), shape((half, BLK, D), BF))] + [gate_grads]
    return call(
        functools.partial(expert_kernel, e),
        "expert_%d" % e,
        (half,),
        [spec((PAIR, D), row), spec((PAIR, D), row), spec((PAIR, 128), row)]
        + [one(w_gate_up), one(w_down)]
        + ([sums[0], gate_grads[0]] if carried else []),
        [o[0] for o in outs],
        [o[1] for o in outs],
        cost(5),
        [] if e else [pltpu.VMEM((FF, D), F32)],
    )(pos, h2, dy_all, gates, w_gate_up, w_down, *carried)


SHARE = 384


def put_shares(out_ref, total):
    for n in range(out_ref.shape[0]):
        out_ref[n] = total[:, n * SHARE : (n + 1) * SHARE].astype(BF)


def by_group(shares, groups):
    cols = D // groups
    if cols == SHARE:
        return shares
    whole = jnp.moveaxis(shares, 0, 1).reshape(FF, groups, cols)
    return jnp.moveaxis(whole, 1, 0)


def down_grad_kernel(pos_ref, ag_ref, dy_ref, out_ref):
    put_shares(out_ref, dot(ag_ref[...], dy_ref[...], 0, 0))


def down_grad(pos, ag, dy_all, groups):
    seq = dy_all.shape[0]
    out = call(
        down_grad_kernel,
        "down_grad",
        (D // (2 * SHARE),),
        [resident(ag.shape), spec((seq, 2 * SHARE), lambda s, pos: (0, s))],
        spec((2, FF, SHARE), lambda s, pos: (s, 0, 0)),
        shape((D // SHARE, FF, SHARE), BF),
        SHORT,
    )(pos, ag, dy_all)
    return by_group(out, groups)


def up_grad_kernel(pos_ref, h2_ref, dgu_ref, out_ref):
    out_ref[...] = dot(h2_ref[...], dgu_ref[...], 0, 0).astype(BF)


def up_grad(pos, h2, dgu):
    seq = h2.shape[0]
    rows = 384
    return call(
        up_grad_kernel,
        "up_grad",
        (D // rows,),
        [spec((seq, rows), lambda s, pos: (0, s)), resident(dgu.shape)],
        spec((rows, 2 * FF), lambda s, pos: (s, 0)),
        shape((D, 2 * FF), BF),
        SHORT,
    )(pos, h2, dgu)


def combine_kernel(pos_ref, *refs):
    ags = refs[:EXP_DEV]
    down_ref, give_ref, keep_ref = refs[EXP_DEV:]
    for h, rows in enumerate(halves(pos_ref)):
        total = dot(ags[0][rows], down_ref[0], 1, 0)
        for e in range(1, EXP_DEV):
            total = total + dot(ags[e][rows], down_ref[e], 1, 0)
        (keep_ref if h else give_ref)[0] = total.astype(BF)


def combine(pos, ags, w_down):
    seq = ags[0].shape[0]
    half = seq // PAIR
    pair = lambda s, pos: (far_pair(s, pos), 0, 0)
    return call(
        combine_kernel,
        "combine",
        (half,),
        [spec((PAIR, FF), lambda s, pos: (s, 0)) for _ in ags] + [resident(w_down.shape)],
        [spec((1, BLK, D), pair), spec((1, BLK, D), pair)],
        [shape((half, BLK, D), BF), shape((half, BLK, D), BF)],
        SHORT,
    )(pos, *ags, w_down)


def norm_pull(values, gain, grad):
    scale = lax.rsqrt(jnp.mean(values * values, axis=1, keepdims=True) + EPSILON)
    unit = values * scale
    inner = grad * gain
    pulled = scale * (inner - unit * jnp.mean(inner * unit, axis=1, keepdims=True))
    return pulled, jnp.sum(grad * unit, axis=0, keepdims=True)


def middle_kernel(
    members, groups, wide, pos_ref, keep_ref, got_ref, fx_ref, fy_ref, fd_ref, y1_ref, h2_ref, gates_ref, dg_ref, dy_ref,
    route_ref, gain_ref, w_ref, dy1_ref, db_ref, da_ref, router_ref, gain_grad_ref,
):
    dh2 = (
        keep_ref[0].astype(F32)
        + got_ref[0].astype(F32)
        + fx_ref[...].astype(F32)
        + fy_ref[...].astype(F32)
        + fd_ref[...].astype(F32)
    )
    gates, gate_grads = gates_ref[...], dg_ref[...]
    mean = jnp.sum(gates * gate_grads, axis=1, keepdims=True)
    dlogits = (gates * (gate_grads - mean)).astype(BF)
    dh2 = dh2 + dot(dlogits, route_ref[...], 1, 1)
    router_ref[...] = dot(h2_ref[...], dlogits, 0, 0)
    pulled, gain_grad = norm_pull(y1_ref[...], gain_ref[...], dh2)
    gain_grad_ref[...] = jnp.broadcast_to(gain_grad, gain_grad_ref.shape)
    dy1 = dy_ref[...].astype(F32) + pulled
    dy1_ref[...] = dy1
    db = (RESIDUAL * dy1).astype(BF)
    db_ref[...] = db
    da = dot(w_ref[...], db, 1, 1).astype(BF)
    for j in range(members):
        da_ref[j, :Q_COLS] = da[j * Q_COLS : (j + 1) * Q_COLS]
    if wide:
        cols = Q_COLS // groups
        db_t = (RESIDUAL * dy1).T.astype(BF)
        for j in range(members):
            for i in range(groups):
                at, to = (i * members + j) * cols, Q_COLS + i * cols
                da_ref[j, to : to + cols] = db_t[at : at + cols]


def middle(groups, pos, keep, got, sums, y1, h2, gates, dg, dy, weights, gain, w_full):
    rows = y1.shape[0]
    full = lambda a: resident(a.shape)
    first = pl.BlockSpec((1, rows, D), lambda s, pos: (0, 0, 0), pipeline_mode=pl.Buffered(1))
    members = HEADS * HEAD_DIM // Q_COLS
    wide = Q_COLS // groups % 16 == 0
    both = 2 * Q_COLS if wide else Q_COLS
    dy1, db, sent, router, gain_grad = call(
        functools.partial(middle_kernel, members, groups, wide),
        "middle",
        (1,),
        [first, first]
        + [full(a) for a in (*sums, y1, h2, gates, dg, dy)]
        + [
            pl.BlockSpec((D, 128), lambda s, pos: (0, 2), pipeline_mode=pl.Buffered(1)),
            full(gain),
            full(w_full),
        ],
        [
            resident((rows, D)),
            resident((rows, D)),
            resident((members, both, rows)),
            resident((D, 128)),
            resident((8, D)),
        ],
        [
            shape((rows, D), F32),
            shape((rows, D), BF),
            shape((members, both, rows), BF),
            shape((D, 128), F32),
            shape((8, D), F32),
        ],
        cost(100),
    )(pos, keep, got, *sums, y1, h2, gates, dg, dy, weights, gain, w_full)
    if not wide:
        cols = Q_COLS // groups
        db_t = jnp.moveaxis(db.T.reshape(groups, members, cols, rows), 1, 0)
        sent = jnp.concatenate([sent, db_t.reshape(members, Q_COLS, rows)], axis=1)
    return dy1, sent, router, gain_grad


def back_kernel(
    pos_ref, dq_ref, dk_ref, dv_ref, cos_ref, sin_ref, w_ref, give_ref, keep_ref, packed_ref
):
    cosine, sine = cos_ref[...], -sin_ref[...]
    rows_t = jnp.concatenate(
        [
            turn_rows(dq_ref[...], cosine, sine),
            turn_rows(dk_ref[...], cosine, sine),
            dv_ref[...],
            jnp.zeros((PACK - QKV, PAIR), F32),
        ],
        axis=0,
    ).astype(BF)
    packed_ref[...] = rows_t
    for h, rows in enumerate(halves(pos_ref)):
        total = dot(packed_ref[:, rows], w_ref[...], 0, 1).astype(BF)
        (keep_ref if h else give_ref)[0] = total


def back(pos, dq_t, dk_t, dv_t, cosine, sine, weights):
    seq = dq_t.shape[1]
    half = seq // PAIR
    column = lambda s, pos: (0, s)
    pair = lambda s, pos: (far_pair(s, pos), 0, 0)
    return call(
        back_kernel,
        "back",
        (half,),
        [
            spec((Q_COLS, PAIR), column),
            spec((HEAD_DIM, PAIR), column),
            spec((HEAD_DIM, PAIR), column),
            spec((HALF, PAIR), column),
            spec((HALF, PAIR), column),
            resident(weights.shape),
        ],
        [spec((1, BLK, D), pair), spec((1, BLK, D), pair), spec((PACK, PAIR), column)],
        [
            shape((half, BLK, D), BF),
            shape((half, BLK, D), BF),
            shape((PACK, seq), BF),
        ],
        SHORT,
    )(pos, dq_t, dk_t, dv_t, cosine, sine, weights)


def low_pair(values):
    high = values.astype(BF).astype(F32)
    return high, values - high


def pack_kernel(pos_ref, packed_ref, x_ref, gain_ref, w_ref, router_ref, moe_ref, out_ref, acc):
    step = pl.program_id(0)

    @pl.when(step == 0)
    def _():
        acc[...] = jnp.zeros_like(acc)

    term = None
    for h in range(2):
        here = x_ref[h ^ (pos_ref[0] % 2)].astype(F32)
        normed = (norm_of(here) * gain_ref[...]).astype(BF)
        part = dot(packed_ref[:, h * BLK : (h + 1) * BLK], normed, 1, 0)
        term = part if term is None else term + part
    acc[...] += term

    @pl.when(step == pl.num_programs(0) - 1)
    def _():
        main, rest = acc[:256].T, acc[256:].T
        w_main, w_rest = w_ref[:, :256].astype(F32), w_ref[:, 256:].astype(F32)
        lane = lax.broadcasted_iota(jnp.int32, (D, 128), 1)
        gain_attn = (
            jnp.sum(main * w_main, axis=1, keepdims=True)
            + jnp.sum(rest * w_rest, axis=1, keepdims=True)
        ) / w_rest[:, ROUTE + 16 : ROUTE + 17]
        high, low = low_pair(router_ref[...])
        moe_high, moe_low = low_pair(moe_ref[...].T)
        attn_high, attn_low = low_pair(gain_attn)
        rest = rest + high + pltpu.roll(low, 16, 1)
        for at, column in enumerate((moe_high[:, :1], moe_low[:, :1], attn_high, attn_low)):
            rest = jnp.where(lane == ROUTE + 32 + at, column, rest)
        out_ref[:, :256] = main.astype(BF)
        out_ref[:, 256:] = rest.astype(BF)


def pack(pos, packed, x_rel, gain, weights, router, moe):
    seq = packed.shape[1]
    return call(
        pack_kernel,
        "pack",
        (seq // PAIR,),
        [
            spec((PACK, PAIR), lambda s, pos: (0, s)),
            spec((2, BLK, D), lambda s, pos: (far_pair(s, pos), 0, 0)),
            resident(gain.shape),
            resident(weights.shape),
            resident(router.shape),
            resident(moe.shape),
        ],
        resident((D, PACK)),
        shape((D, PACK), BF),
        cost(50),
        [pltpu.VMEM((PACK, D), F32)],
    )(pos, packed, x_rel, gain, weights, router, moe)


def last_kernel(
    pos_ref, keep_ref, got_ref, fx_ref, fy_ref, fd_ref, x_ref, gain_ref, dy1_ref, out_ref
):
    dh1 = (
        keep_ref[0].astype(F32)
        + got_ref[0].astype(F32)
        + fx_ref[...].astype(F32)
        + fy_ref[...].astype(F32)
        + fd_ref[...].astype(F32)
    )
    pulled, _ = norm_pull(x_ref[...].astype(F32), gain_ref[...], dh1)
    out_ref[...] = (dy1_ref[...] + pulled).astype(BF)


def last(pos, keep, got, sums, x, gain, dy1):
    rows = x.shape[0]
    full = lambda a: resident(a.shape)
    first = pl.BlockSpec((1, rows, D), lambda s, pos: (0, 0, 0), pipeline_mode=pl.Buffered(1))
    return call(
        last_kernel,
        "last",
        (1,),
        [first, first] + [full(a) for a in (*sums, x, gain, dy1)],
        resident((rows, D)),
        shape((rows, D), BF),
        cost(50),
    )(pos, keep, got, *sums, x, gain, dy1)


def out_grad_kernel(count, pos_ref, *refs):
    pieces = refs[: count + 2]
    db_ref, out_ref, heads = refs[count + 2 :]
    step = pl.program_id(0)
    pos = pos_ref[0]
    for r in range(count):
        base = (pos ^ r) * Q_COLS
        if r < count - 2:
            heads[pl.ds(pl.multiple_of(base, Q_COLS), Q_COLS), :] = pieces[r][...]
        else:
            half = Q_COLS // 2
            at = count - 2 + 2 * (r - count + 2)
            heads[pl.ds(pl.multiple_of(base, half), half), :] = pieces[at][...]
            heads[pl.ds(pl.multiple_of(base + half, half), half), :] = pieces[at + 1][...]
    term = dot(db_ref[0], heads[...], 1, 1)

    @pl.when(step == 0)
    def _():
        out_ref[...] = term

    @pl.when(step > 0)
    def _():
        out_ref[...] += term


def out_grad(pos, pieces, came):
    count = len(pieces) - 2
    seq, cols = came.shape[0] * BLK, Q_COLS
    return call(
        functools.partial(out_grad_kernel, count),
        "out_grad",
        (seq // BLK,),
        [spec((a.shape[0], BLK), lambda s, pos: (0, s)) for a in pieces]
        + [spec((1, cols, BLK), lambda s, pos: (s, 1, 0))],
        resident((cols, HEADS * HEAD_DIM)),
        shape((cols, HEADS * HEAD_DIM), F32),
        SHORT,
        [pltpu.VMEM((HEADS * HEAD_DIM, BLK), BF)],
    )(pos, *pieces, came).astype(BF)


def unpack_kernel(groups, members, pos_ref, came_ref, query_ref, pair_ref, rest_ref):
    total = None
    for j in range(members):
        here = came_ref[j].astype(F32)
        for i in range(1, groups):
            here = here + came_ref[i * members + j].astype(F32)
        query_ref[:, j * Q_COLS : (j + 1) * Q_COLS] = here[:, :Q_COLS]
        pair_ref[:, j * HEAD_DIM : (j + 1) * HEAD_DIM] = here[:, Q_COLS : Q_COLS + HEAD_DIM]
        at = (members + j) * HEAD_DIM
        pair_ref[:, at : at + HEAD_DIM] = here[:, Q_COLS + HEAD_DIM : QKV]
        rest = here[:, 256:]
        total = rest if total is None else total + rest
    rest_ref[...] = total


def unpack(pos, came, groups):
    devices, rows, _ = came.shape
    members = devices // groups
    return call(
        functools.partial(unpack_kernel, groups, members),
        "unpack",
        (1,),
        [resident(came.shape)],
        [resident((rows, D)), resident((rows, 2 * KV_HEADS * HEAD_DIM)), resident((rows, 128))],
        [
            shape((rows, D), F32),
            shape((rows, 2 * KV_HEADS * HEAD_DIM), F32),
            shape((rows, 128), F32),
        ],
        SHORT,
    )(pos, came)


def swap(values, bit):
    count = lax.axis_size("expert")
    return lax.ppermute(values, "expert", [(i, i ^ bit) for i in range(count)])


def gather_pieces(own, before_last):
    half = own.shape[0] // 2
    x, y = swap(own, 2), swap(own, 4)
    core = swap(own, 1)
    far_a, far_b = tie((swap(x[:half], 4), swap(y[half:], 2)), before_last)
    return [
        own, core, x, swap(x, 1), y, swap(y, 1),
        far_a, far_b, swap(far_a, 1), swap(far_b, 1),
    ]


def gather_direct(own):
    near = [own, swap(own, 2), swap(own, 4), swap(own, 6)]
    return [piece for value in near for piece in (value, swap(value, 1))]


def tie(values, *after):
    return lax.optimization_barrier((values, after))[0]


def pair_sums(keep, got):
    return [(keep[r].astype(F32) + got[r].astype(F32)).astype(BF) for r in (1, 2, 3)]


def send_sums(sums):
    return [swap(sums[0], 2), swap(sums[1], 4), swap(sums[2], 6)]


def send_to_groups(blocks):
    count = lax.axis_size("dp")
    me = lax.axis_index("dp")
    terms = [lax.dynamic_index_in_dim(blocks, me, 0, False)]
    for k in range(1, count):
        sent = lax.dynamic_index_in_dim(blocks, (me + k) % count, 0, False)
        terms.append(lax.ppermute(sent, "dp", [(i, (i + k) % count) for i in range(count)]))
    return terms


def exchange(blocks, axes):
    return lax.all_to_all(blocks, axes, split_axis=0, concat_axis=0, tiled=True)


def shards(
    tokens,
    segment_ids,
    expert_ids,
    w_query,
    w_key_value,
    w_out,
    w_router,
    norm_attn,
    norm_moe,
    w_gate_up,
    w_down,
    grad_out,
):
    tok_rows = tokens.shape[0]
    members = lax.axis_size("expert")
    groups = lax.axis_size("dp")
    position = lax.axis_index("expert")
    pos = position.astype(jnp.int32).reshape(1)
    devices = groups * members
    seq = tok_rows * members
    expert_total = EXP_DEV * members
    in_rows = w_query.shape[0]
    out_cols = w_out.shape[1]
    kv_cols = KV_HEADS * HEAD_DIM

    start = jnp.sum(
        (segment_ids[:, None] < segment_ids[None, :]).astype(jnp.int32), axis=0, keepdims=True
    )
    first = jnp.stack([start[0, ::BLK] // BLK, (start[0, BLK - 1 :: BLK] + BLK - 1) // BLK])
    x_pieces = gather_pieces(tokens, (start, first))

    rest = jnp.concatenate(
        [
            w_router,
            norm_attn[:, None],
            norm_moe[:, None],
            jnp.zeros((in_rows, PACK - QKV - expert_total - 2), BF),
        ],
        axis=1,
    )
    own = send_weights(pos, w_query, w_key_value, rest, groups, members)
    weights = exchange(own, BOTH).reshape(D, PACK)
    gain_attn = weights[:, QKV + expert_total].astype(F32)[None]
    gain_moe = weights[:, QKV + expert_total + 1].astype(F32)[None]

    token_pos = jnp.arange(seq, dtype=jnp.int32)
    frequency = ROPE_BASE ** (-(jnp.arange(HALF, dtype=F32) * 2.0 / HEAD_DIM))
    angles = frequency[:, None] * token_pos.astype(F32)[None, :]
    cosine, sine = jnp.cos(angles), jnp.sin(angles)

    q_t, k_t, v_t, k, v = qkv_forward(
        pos, x_pieces, weights, gain_attn, cosine, sine
    )
    w_full = lax.all_gather(tie(w_out.T, own), BOTH, axis=0, tiled=True)
    dy_all = lax.all_gather(tie(grad_out, own), "expert", axis=0, tiled=True)
    w_full = w_full.T
    a_t, o_t, lse = attn_forward(first, q_t, k, v_t, start)
    ids = jnp.concatenate(gather_direct(tie(expert_ids, q_t).T), axis=0)
    ids = ids.reshape(members, TOP, tok_rows)
    a_pieces = gather_pieces(a_t, (w_full, ids))
    x_rel = jnp.concatenate(tie(x_pieces, a_t), axis=0).reshape(members, tok_rows, D)

    h2, gates, y1, h2_own, gates_own = mix_forward(
        pos, a_pieces, x_rel, w_full, gain_moe, weights, ids
    )

    ag0, dgu0, *carried, down0 = expert_pass(0, pos, h2, dy_all, gates, w_gate_up, w_down)
    down0 = by_group(down0, groups)
    ag1, dgu1, give, keep, dg = expert_pass(
        1, pos, h2, dy_all, gates, w_gate_up, w_down, carried
    )
    got = swap(give, 1)
    down1 = down_grad(pos, ag1, dy_all, groups)
    sums = pair_sums(keep, tie(got, down1))
    came_sums = send_sums(sums)
    dg = exchange(tie(dg, sums), "expert")[:, :EXP_DEV].reshape(expert_total, tok_rows).T
    dg = jnp.pad(dg, ((0, 0), (ROUTE, 128 - ROUTE - expert_total)))
    up0 = up_grad(pos, *tie((h2, dgu0), sums))
    up1 = up_grad(pos, *tie((h2, dgu1), up0))
    out_give, out_keep = combine(pos, tie((ag0, ag1), up1), w_down)
    spread = functools.partial(lax.psum_scatter, axis_name="dp", scatter_dimension=0, tiled=True)
    down_share = [spread(d.reshape(groups * FF, -1)) for d in (down0, down1)]
    up_share = [spread(d) for d in (up0, up1)]
    keep, down_share[0] = lax.optimization_barrier((keep, down_share[0]))
    out_got = swap(out_give, 1)

    dy1, da, router_wgrad, moe_gain_grad = middle(
        groups, pos, tie(keep, out_keep), got, came_sums, y1, h2_own, gates_own, dg, grad_out,
        weights, gain_moe, w_full,
    )
    da = exchange(da, "expert")
    out_sums = pair_sums(out_keep, tie(out_got, dy1))
    out_came = send_sums(out_sums)

    dq_t, dk_t, dv_t = attn_backward(first, q_t, tie(da, out_sums), o_t, lse, k, k_t, v, start)
    give1, keep1, packed = back(pos, dq_t, dk_t, dv_t, cosine, sine, weights)
    got1 = swap(give1, 1)
    sent = pack(pos, packed, x_rel, gain_attn, weights, router_wgrad, moe_gain_grad)
    sums1 = pair_sums(keep1, tie(got1, sent))
    came_sums1 = send_sums(sums1)
    result = y1 + out_keep[0].astype(F32) + out_got[0].astype(F32)
    for term in tie(out_came, sums1):
        result = result + term.astype(F32)
    result = result.astype(BF)
    out_wgrad = out_grad(pos, a_pieces, tie(da, result)).reshape(groups, out_cols, D)
    out_terms = send_to_groups(out_wgrad)
    came = exchange(sent.reshape(devices, in_rows, PACK), BOTH)
    token_grad = last(pos, keep1, got1, came_sums1, tokens, gain_attn, dy1)
    query_share, pair_share, rest = unpack(pos, tie(came, token_grad), groups)
    router_share = (
        rest[:, ROUTE : ROUTE + expert_total]
        + rest[:, ROUTE + expert_total : ROUTE + 2 * expert_total]
    )
    moe_gain_share = rest[:, ROUTE + 32] + rest[:, ROUTE + 33]

    attn_gain_share = rest[:, ROUTE + 34] + rest[:, ROUTE + 35]
    out_share = sum(term.astype(F32) for term in tie(out_terms, token_grad)).T

    return (
        result,
        token_grad,
        query_share,
        pair_share,
        out_share,
        router_share,
        attn_gain_share,
        moe_gain_share,
        jnp.stack(tie(up_share, rest, out_share)).astype(F32),
        jnp.stack(down_share).astype(F32),
    )


def solution(mesh):
    in_specs = (
        P(("dp", "expert"), None),
        P("dp"),
        P(("dp", "expert"), None),
        P(("dp", "expert"), None),
        P(("dp", "expert"), None),
        P(None, ("dp", "expert")),
        P(("dp", "expert"), None),
        P(("dp", "expert")),
        P(("dp", "expert")),
        P("expert", None, None),
        P("expert", None, None),
        P(("dp", "expert"), None),
    )
    out_specs = (
        P(("dp", "expert"), None),
        P(("dp", "expert"), None),
        P(("dp", "expert"), None),
        P(("dp", "expert"), None),
        P(None, ("dp", "expert")),
        P(("dp", "expert"), None),
        P(("dp", "expert")),
        P(("dp", "expert")),
        P("expert", "dp", None),
        P("expert", None, "dp"),
    )
    return jax.shard_map(shards, mesh=mesh, in_specs=in_specs, out_specs=out_specs, check_vma=False)
```

profile of v0, /device:TPU:0, one launch (start us, length us, event | category | flops | bytes accessed | tf_op | source)
XLA Modules:
  0.0 458.8 jit_solution(11693319590427319363)
XLA Ops:
  12.5 7.3 %all-to-all-start = ((bf16[32,48,384]{2,1,0:T(8,128)(2,1)}), bf16[32,48,384]{2,1,0:T(8,128)(2,1)S(1)}, u32[]{:S(2)}, u32[]{:S(2)}) async-start(bf16[32,48,384]{2,1,0:T(8,128)(2,1)} %send_weights.1), calls=%async_computation | async-start | bytes 2359296 | tf_op jit(solution)/shard_map/all_to_all | solution.py:937
  25.5 29.8 %collective-permute-done.3.refs_4_ = bf16[256,1536]{1,0:T(8,128)(2,1)S(1)} collective-permute-done((bf16[256,1536]{1,0:T(8,128)(2,1)}, bf16[256,1536]{1,0:T(8,128)(2,1)S(1)}, u32[]{:S(2)}, u32[]{:S(2)}) %collective-permute-start.3) | collective-permute-done | bytes 786464 | tf_op jit(solution)/shard_map/ppermute | solution.py:895
  60.2 6.1 %collective-permute-done.6.refs_7_ = bf16[128,1536]{1,0:T(8,128)(2,1)} collective-permute-done((bf16[128,1536]{1,0:T(8,128)(2,1)S(1)}, bf16[128,1536]{1,0:T(8,128)(2,1)}, u32[]{:S(2)}, u32[]{:S(2)}) %collective-permute-start.6) | collective-permute-done | bytes 393248 | tf_op jit(solution)/shard_map/ppermute | solution.py:895
  73.0 9.2 %qkv.1 = (bf16[192,2048]{1,0:T(8,128)(2,1)}, bf16[64,2048]{1,0:T(8,128)(2,1)}, bf16[64,2048]{1,0:T(8,128)(2,1)}, bf16[2048,64]{1,0:T(8,128)(2,1)}, bf16[2048,64]{1,0:T(8,128)(2,1)}) custom-call(s32[1]{0:T(128)} %bitcast.pos_ref, bf16[256,1536]{1,0:T(8,128)(2,1)} %x_ref.1, bf16[256,1536]{1,0:T(8,128)(2,1)} %collective-permute-done.refs_1_, ...), custom_call_target="tpu_custom_call" | custom-call | flops 399999991808 | bytes 10000 | tf_op jit(solution)/shard_map/qkv/pallas_call | solution.py:324
  84.7 18.9 %attn_fwd.1 = (bf16[192,2048]{1,0:T(8,128)(2,1)}, f32[192,2048]{1,0:T(8,128)}, f32[8,2048]{1,0:T(8,128)}) custom-call(s32[2,8]{1,0:T(2,128)} %pad_add_fusion.first_ref, bf16[192,2048]{1,0:T(8,128)(2,1)} %get-tuple-element.92.q_ref, bf16[2048,64]{1,0:T(8,128)(2,1)} %get-tuple-element.93.k_ref, bf16[64,2048]{1,0:T(8,128)(2,1)} %get-tuple-element.94.vt_ref, ...), custom_call_target="tpu_custom_call" | custom-call | flops 49999998976 | bytes 10000 | tf_op jit(solution)/shard_map/attn_fwd/pallas_call | solution.py:168
  116.7 13.0 %collective-permute-done.19 = s32[8,256]{1,0:T(8,128)S(1)} collective-permute-done((s32[8,256]{1,0:T(8,128)S(1)}, s32[8,256]{1,0:T(8,128)S(1)}, u32[]{:S(2)}, u32[]{:S(2)}) %collective-permute-start.19) | collective-permute-done | bytes 8224 | tf_op jit(solution)/shard_map/ppermute | solution.py:895
  137.4 6.7 %copy.43 = bf16[1536,1536]{0,1:T(8,128)(2,1)} copy(bf16[1536,1536]{1,0:T(8,128)(2,1)} %all-gather.3.cloned.1.call-done) | data formatting | bytes 9437184 | tf_op jit(solution)/shard_map/all_gather | solution.py:994
  144.1 5.9 %collective-permute-done.15.refs_7_ = bf16[96,2048]{1,0:T(8,128)(2,1)S(1)} collective-permute-done((bf16[96,2048]{1,0:T(8,128)(2,1)}, bf16[96,2048]{1,0:T(8,128)(2,1)S(1)}, u32[]{:S(2)}, u32[]{:S(2)}) %collective-permute-start.15) | collective-permute-done | bytes 393248 | tf_op jit(solution)/shard_map/ppermute | solution.py:895
  155.7 22.8 %mix.1 = (bf16[2048,1536]{1,0:T(8,128)(2,1)}, f32[2048,128]{1,0:T(8,128)}, f32[256,1536]{1,0:T(8,128)}, bf16[256,1536]{1,0:T(8,128)(2,1)}, f32[256,128]{1,0:T(8,128)}) custom-call(s32[1]{0:T(128)} %bitcast.pos_ref, bf16[192,2048]{1,0:T(8,128)(2,1)} %get-tuple-element.95.refs_0_, bf16[192,2048]{1,0:T(8,128)(2,1)} %copy-done.12, bf16[192,2048]{1,0:T(8,128)(2,1)} %copy-done.5, ...), custom_call_target="tpu_custom_call" | custom-call | flops 49999998976 | bytes 10000 | tf_op jit(solution)/shard_map/mix/pallas_call | solution.py:414
  178.5 29.9 %expert_0.1 = (bf16[2048,512]{1,0:T(8,128)(2,1)}, bf16[2048,1024]{1,0:T(8,128)(2,1)}, f32[2048,1536]{1,0:T(8,128)}, f32[8,8,256]{2,1,0:T(8,128)}, bf16[4,512,384]{2,1,0:T(8,128)(2,1)}) custom-call(s32[1]{0:T(128)} %bitcast.pos_ref, bf16[2048,1536]{1,0:T(8,128)(2,1)} %get-tuple-element.125.h2_ref, bf16[2048,1536]{1,0:T(8,128)(2,1)} %all-gather.5.cloned.1.call-done.dy_ref, ...), custom_call_target="tpu_custom_call" | custom-call | flops 5000000000 | bytes 10000 | tf_op jit(solution)/shard_map/expert_0/pallas_call | solution.py:510
  208.4 26.1 %expert_1.1 = (bf16[2048,512]{1,0:T(8,128)(2,1)}, bf16[2048,1024]{1,0:T(8,128)(2,1)}, bf16[4,256,1536]{2,1,0:T(8,128)(2,1)}, bf16[4,256,1536]{2,1,0:T(8,128)(2,1)}, f32[8,8,256]{2,1,0:T(8,128)}) custom-call(s32[1]{0:T(128)} %bitcast.pos_ref, bf16[2048,1536]{1,0:T(8,128)(2,1)} %get-tuple-element.125.h2_ref, ...), custom_call_target="tpu_custom_call" | custom-call | flops 5000000000 | bytes 10000 | tf_op jit(solution)/shard_map/expert_1/pallas_call | solution.py:510
  234.7 7.3 %down_grad.1 = bf16[4,512,384]{2,1,0:T(8,128)(2,1)} custom-call(s32[1]{0:T(128)} %bitcast.pos_ref, bf16[2048,512]{1,0:T(8,128)(2,1)} %get-tuple-element.128.ag_ref.refs_1_, bf16[2048,1536]{1,0:T(8,128)(2,1)} %all-gather.5.cloned.1.call-done.dy_ref), custom_call_target="tpu_custom_call" | custom-call | bytes 10000 | tf_op jit(solution)/shard_map/down_grad/pallas_call | solution.py:546
  252.4 11.1 %up_grad.2 = bf16[1536,1024]{1,0:T(8,128)(2,1)} custom-call(s32[1]{0:T(128)} %bitcast.pos_ref, bf16[2048,1536]{1,0:T(8,128)(2,1)} %get-tuple-element.125.h2_ref, bf16[2048,1024]{1,0:T(8,128)(2,1)} %get-tuple-element.124.dgu_ref), custom_call_target="tpu_custom_call" | custom-call | bytes 10000 | tf_op jit(solution)/shard_map/up_grad/pallas_call | solution.py:565
  263.5 11.0 %up_grad.3 = bf16[1536,1024]{1,0:T(8,128)(2,1)} custom-call(s32[1]{0:T(128)} %bitcast.pos_ref, bf16[2048,1536]{1,0:T(8,128)(2,1)} %get-tuple-element.125.h2_ref, bf16[2048,1024]{1,0:T(8,128)(2,1)} %get-tuple-element.126.dgu_ref), custom_call_target="tpu_custom_call" | custom-call | bytes 10000 | tf_op jit(solution)/shard_map/up_grad/pallas_call | solution.py:565
  274.4 10.6 %combine.1 = (bf16[4,256,1536]{2,1,0:T(8,128)(2,1)}, bf16[4,256,1536]{2,1,0:T(8,128)(2,1)}) custom-call(s32[1]{0:T(128)} %bitcast.pos_ref, bf16[2048,512]{1,0:T(8,128)(2,1)} %get-tuple-element.127.refs_0_, bf16[2048,512]{1,0:T(8,128)(2,1)} %get-tuple-element.128.ag_ref.refs_1_, bf16[2,512,1536]{2,1,0:T(8,128)(2,1)} %refs_2_.1), custom_call_target="tpu_custom_call" | custom-call | bytes 10000 | tf_op jit(solution)/shard_map/combine/pallas_call | solution.py:590
  287.7 8.7 %middle.1 = (f32[256,1536]{1,0:T(8,128)}, bf16[256,1536]{1,0:T(8,128)(2,1)}, bf16[8,384,256]{2,1,0:T(8,128)(2,1)}, f32[1536,128]{1,0:T(8,128)}, f32[8,1536]{1,0:T(8,128)}) custom-call(s32[1]{0:T(128)} %bitcast.pos_ref, bf16[4,256,1536]{2,1,0:T(8,128)(2,1)} %get-tuple-element.133.keep_ref, bf16[4,256,1536]{2,1,0:T(8,128)(2,1)} %collective-permute-done.25.got_ref, ...), custom_call_target="tpu_custom_call" | custom-call | flops 99999997952 | bytes 10000 | tf_op jit(solution)/shard_map/middle/pallas_call | solution.py:650
  310.8 11.2 %all-to-all-done.2.da_ref.refs_10_ = bf16[8,384,256]{2,1,0:T(8,128)(2,1)S(1)} async-done(((bf16[8,384,256]{2,1,0:T(8,128)(2,1)}), bf16[8,384,256]{2,1,0:T(8,128)(2,1)S(1)}, u32[]{:S(2)}, u32[]{:S(2)}) %all-to-all-start.2) | async-done | bytes 1572896 | tf_op jit(solution)/shard_map/all_to_all | solution.py:937
  323.2 26.9 %attn_bwd.1 = (f32[192,2048]{1,0:T(8,128)}, f32[64,2048]{1,0:T(8,128)}, f32[64,2048]{1,0:T(8,128)}) custom-call(s32[2,8]{1,0:T(2,128)} %pad_add_fusion.first_ref, bf16[192,2048]{1,0:T(8,128)(2,1)} %get-tuple-element.92.q_ref, bf16[8,384,256]{2,1,0:T(8,128)(2,1)} %copy-done.1, f32[192,2048]{1,0:T(8,128)} %get-tuple-element.142.o_ref, ...), custom_call_target="tpu_custom_call" | custom-call | flops 20000000000 | bytes 10000 | tf_op jit(solution)/shard_map/attn_bwd/pallas_call | solution.py:200
  350.1 7.8 %back.1 = (bf16[4,256,1536]{2,1,0:T(8,128)(2,1)}, bf16[4,256,1536]{2,1,0:T(8,128)(2,1)}, bf16[384,2048]{1,0:T(8,128)(2,1)}) custom-call(s32[1]{0:T(128)} %bitcast.pos_ref, f32[192,2048]{1,0:T(8,128)} %get-tuple-element.146.dq_ref, f32[64,2048]{1,0:T(8,128)} %get-tuple-element.147.dk_ref, f32[64,2048]{1,0:T(8,128)} %get-tuple-element.148.dv_ref, ...), custom_call_target="tpu_custom_call" | custom-call | bytes 10000 | tf_op jit(solution)/shard_map/back/pallas_call | solution.py:708
  357.9 10.3 %pack.1 = bf16[1536,384]{1,0:T(8,128)(2,1)} custom-call(s32[1]{0:T(128)} %bitcast.pos_ref, bf16[384,2048]{1,0:T(8,128)(2,1)} %get-tuple-element.151.packed_ref, bf16[8,256,1536]{2,1,0:T(8,128)(2,1)} %bitcast.75, f32[1,1536]{1,0:T(1,128)} %reshape.134.refs_11_.gain_ref, bf16[1536,384]{1,0:T(8,128)(2,1)} %bitcast.61, ...), custom_call_target="tpu_custom_call" | custom-call | flops 49999998976 | bytes 10000 | tf_op jit(solution)/shard_map/pack/pallas_call | solution.py:771
  381.9 9.0 %out_grad.1 = f32[192,1536]{1,0:T(8,128)} custom-call(s32[1]{0:T(128)} %bitcast.pos_ref, bf16[192,2048]{1,0:T(8,128)(2,1)} %get-tuple-element.95.refs_0_, bf16[192,2048]{1,0:T(8,128)(2,1)} %copy-done.12, bf16[192,2048]{1,0:T(8,128)(2,1)} %copy-done.5, bf16[192,2048]{1,0:T(8,128)(2,1)} %collective-permute-done.11.refs_3_, bf16[192,2048]{1,0:T(8,128)(2,1)} %copy-done.4, ...), custom_call_target="tpu_custom_call" | custom-call | bytes 10000 | tf_op jit(solution)/shard_map/out_grad/pallas_call | solution.py:847
  395.9 9.4 %collective-permute-done.36.fd_ref = bf16[256,1536]{1,0:T(8,128)(2,1)} collective-permute-done((bf16[256,1536]{1,0:T(8,128)(2,1)}, bf16[256,1536]{1,0:T(8,128)(2,1)}, u32[]{:S(2)}, u32[]{:S(2)}) %collective-permute-start.36) | collective-permute-done | bytes 786464 | tf_op jit(solution)/shard_map/ppermute | solution.py:895
  405.4 16.7 %collective-permute-done.35.fy_ref = bf16[256,1536]{1,0:T(8,128)(2,1)} collective-permute-done((bf16[256,1536]{1,0:T(8,128)(2,1)}, bf16[256,1536]{1,0:T(8,128)(2,1)}, u32[]{:S(2)}, u32[]{:S(2)}) %collective-permute-start.35) | collective-permute-done | bytes 786464 | tf_op jit(solution)/shard_map/ppermute | solution.py:895
  428.7 12.6 %collective-permute-done.38 = bf16[48,1536]{1,0:T(8,128)(2,1)S(1)} collective-permute-done((bf16[48,1536]{1,0:T(8,128)(2,1)S(1)}, bf16[48,1536]{1,0:T(8,128)(2,1)S(1)}, u32[]{:S(2)}, u32[]{:S(2)}) %collective-permute-start.38) | collective-permute-done | bytes 147488 | tf_op jit(solution)/shard_map/ppermute | solution.py:932
  (209 shorter events, 115.6 us)
Async XLA Ops:
  7.2 130.2 %all-gather.3.cloned.1.call-start = ((), (), s32[]{:S(2)}) async-start(), calls=%async_computation.8 | async-start | bytes 4866048 | tf_op jit(solution)/shard_map/all_gather | solution.py:994
  12.5 58.0 %all-to-all-start = ((bf16[32,48,384]{2,1,0:T(8,128)(2,1)}), bf16[32,48,384]{2,1,0:T(8,128)(2,1)S(1)}, u32[]{:S(2)}, u32[]{:S(2)}) async-start(bf16[32,48,384]{2,1,0:T(8,128)(2,1)} %send_weights.1), calls=%async_computation | async-start | bytes 2359296 | tf_op jit(solution)/shard_map/all_to_all | solution.py:937
  19.8 158.7 %all-gather.5.cloned.1.call-start = ((), (), s32[]{:S(2)}) async-start(), calls=%async_computation.9 | async-start | bytes 7077888 | tf_op jit(solution)/shard_map/all_gather | solution.py:995
  19.8 35.5 %collective-permute-start.3 = (bf16[256,1536]{1,0:T(8,128)(2,1)}, bf16[256,1536]{1,0:T(8,128)(2,1)S(1)}, u32[]{:S(2)}, u32[]{:S(2)}) collective-permute-start(bf16[256,1536]{1,0:T(8,128)(2,1)} %x_ref.1), channel_id=1, source_target_pairs={{0,4},{1,5},{2,6},{3,7},{4,0},{5,1},{6,2},{7,3},{8,12},{9,13},{10,... | collective-permute-start | bytes 2359304 | tf_op jit(solution)/shard_map/ppermute | solution.py:895
  21.7 35.7 %collective-permute-start.1 = (bf16[256,1536]{1,0:T(8,128)(2,1)}, bf16[256,1536]{1,0:T(8,128)(2,1)S(1)}, u32[]{:S(2)}, u32[]{:S(2)}) collective-permute-start(bf16[256,1536]{1,0:T(8,128)(2,1)} %x_ref.1), channel_id=1, source_target_pairs={{0,2},{1,3},{2,0},{3,1},{4,6},{5,7},{6,4},{7,5},{8,10},{9,11},{10,... | collective-permute-start | bytes 2359304 | tf_op jit(solution)/shard_map/ppermute | solution.py:895
  23.1 49.0 %collective-permute-start = (bf16[256,1536]{1,0:T(8,128)(2,1)}, bf16[256,1536]{1,0:T(8,128)(2,1)}, u32[]{:S(2)}, u32[]{:S(2)}) collective-permute-start(bf16[256,1536]{1,0:T(8,128)(2,1)} %x_ref.1), channel_id=1, source_target_pairs={{0,1},{1,0},{2,3},{3,2},{4,5},{5,4},{6,7},{7,6},{8,9},{9,8},{10,11... | collective-permute-start | bytes 2359304 | tf_op jit(solution)/shard_map/ppermute | solution.py:895
  23.1 229.2 %reduce-scatter.5.cloned.1.call-start = ((), (), s32[]{:S(2)}) async-start(), calls=%async_computation.10 | async-start | bytes 1966080 | tf_op jit(solution)/shard_map/reduce_scatter | solution.py:1022
  116.2 37.9 %collective-permute-start.9 = (bf16[192,2048]{1,0:T(8,128)(2,1)S(1)}, bf16[192,2048]{1,0:T(8,128)(2,1)S(1)}, u32[]{:S(2)}, u32[]{:S(2)}) collective-permute-start(bf16[192,2048]{1,0:T(8,128)(2,1)S(1)} %copy-done.11), channel_id=1, source_target_pairs={{0,1},{1,0},{2,3},{3,2},{4,5},{5,4},{6,7},{7,6},{8,9},{9,8},{10,11... | collective-permute-start | bytes 2359304 | tf_op jit(solution)/shard_map/ppermute | solution.py:895
  208.4 92.6 %reduce-scatter.11.cloned.1.call-start = ((), (), s32[]{:S(2)}) async-start(), calls=%async_computation.13 | async-start | bytes 1966080 | tf_op jit(solution)/shard_map/reduce_scatter | solution.py:1022
  245.4 40.9 %collective-permute-start.29 = (bf16[256,1536]{1,0:T(8,128)(2,1)}, bf16[256,1536]{1,0:T(8,128)(2,1)S(1)}, u32[]{:S(2)}, u32[]{:S(2)}) collective-permute-start(bf16[256,1536]{1,0:T(8,128)(2,1)} %get-tuple-element.220), channel_id=1, source_target_pairs={{0,6},{1,7},{2,4},{3,5},{4,2},{5,3},{6,0},{7,1},{8,14},{9,15},{10,... | collective-permute-start | bytes 2359304 | tf_op jit(solution)/shard_map/ppermute | solution.py:895
  246.9 39.4 %collective-permute-start.28 = (bf16[256,1536]{1,0:T(8,128)(2,1)}, bf16[256,1536]{1,0:T(8,128)(2,1)S(1)}, u32[]{:S(2)}, u32[]{:S(2)}) collective-permute-start(bf16[256,1536]{1,0:T(8,128)(2,1)} %get-tuple-element.221), channel_id=1, source_target_pairs={{0,4},{1,5},{2,6},{3,7},{4,0},{5,1},{6,2},{7,3},{8,12},{9,13},{10,... | collective-permute-start | bytes 2359304 | tf_op jit(solution)/shard_map/ppermute | solution.py:895
  248.3 38.0 %collective-permute-start.27 = (bf16[256,1536]{1,0:T(8,128)(2,1)}, bf16[256,1536]{1,0:T(8,128)(2,1)S(1)}, u32[]{:S(2)}, u32[]{:S(2)}) collective-permute-start(bf16[256,1536]{1,0:T(8,128)(2,1)} %get-tuple-element.222), channel_id=1, source_target_pairs={{0,2},{1,3},{2,0},{3,1},{4,6},{5,7},{6,4},{7,5},{8,10},{9,11},{10,... | collective-permute-start | bytes 2359304 | tf_op jit(solution)/shard_map/ppermute | solution.py:895
  248.9 36.5 %all-to-all-start.1 = ((f32[8,8,256]{2,1,0:T(8,128)}), f32[8,8,256]{2,1,0:T(8,128)S(1)}, u32[]{:S(2)}, u32[]{:S(2)}) async-start(f32[8,8,256]{2,1,0:T(8,128)} %get-tuple-element.137), calls=%async_computation.2 | async-start | bytes 131072 | tf_op jit(solution)/shard_map/all_to_all | solution.py:937
  252.3 195.5 %reduce-scatter.9.cloned.1.call-start = ((), (), s32[]{:S(2)}) async-start(), calls=%async_computation.12 | async-start | bytes 3932160 | tf_op jit(solution)/shard_map/reduce_scatter | solution.py:1023
  300.4 147.4 %reduce-scatter.7.cloned.1.call-start = ((), (), s32[]{:S(2)}) async-start(), calls=%async_computation.11 | async-start | bytes 3932160 | tf_op jit(solution)/shard_map/reduce_scatter | solution.py:1023
  307.3 70.9 %collective-permute-start.32 = (bf16[256,1536]{1,0:T(8,128)(2,1)}, bf16[256,1536]{1,0:T(8,128)(2,1)S(1)}, u32[]{:S(2)}, u32[]{:S(2)}) collective-permute-start(bf16[256,1536]{1,0:T(8,128)(2,1)} %get-tuple-element.217), channel_id=1, source_target_pairs={{0,6},{1,7},{2,4},{3,5},{4,2},{5,3},{6,0},{7,1},{8,14},{9,15},{10,... | collective-permute-start | bytes 2359304 | tf_op jit(solution)/shard_map/ppermute | solution.py:895
  310.2 68.4 %collective-permute-start.31 = (bf16[256,1536]{1,0:T(8,128)(2,1)}, bf16[256,1536]{1,0:T(8,128)(2,1)S(1)}, u32[]{:S(2)}, u32[]{:S(2)}) collective-permute-start(bf16[256,1536]{1,0:T(8,128)(2,1)} %get-tuple-element.218), channel_id=1, source_target_pairs={{0,4},{1,5},{2,6},{3,7},{4,0},{5,1},{6,2},{7,3},{8,12},{9,13},{10,... | collective-permute-start | bytes 2359304 | tf_op jit(solution)/shard_map/ppermute | solution.py:895
  310.8 67.8 %collective-permute-start.30 = (bf16[256,1536]{1,0:T(8,128)(2,1)}, bf16[256,1536]{1,0:T(8,128)(2,1)}, u32[]{:S(2)}, u32[]{:S(2)}) collective-permute-start(bf16[256,1536]{1,0:T(8,128)(2,1)} %get-tuple-element.219), channel_id=1, source_target_pairs={{0,2},{1,3},{2,0},{3,1},{4,6},{5,7},{6,4},{7,5},{8,10},{9,11},{10,... | collective-permute-start | bytes 2359304 | tf_op jit(solution)/shard_map/ppermute | solution.py:895
  368.3 73.0 %all-to-all-start.3 = ((bf16[32,48,384]{2,1,0:T(8,128)(2,1)}), bf16[32,48,384]{2,1,0:T(8,128)(2,1)S(1)}, u32[]{:S(2)}, u32[]{:S(2)}) async-start(bf16[32,48,384]{2,1,0:T(8,128)(2,1)} %bitcast.67), calls=%async_computation.4 | async-start | bytes 2359296 | tf_op jit(solution)/shard_map/all_to_all | solution.py:937
  377.7 44.3 %collective-permute-start.35 = (bf16[256,1536]{1,0:T(8,128)(2,1)}, bf16[256,1536]{1,0:T(8,128)(2,1)}, u32[]{:S(2)}, u32[]{:S(2)}) collective-permute-start(bf16[256,1536]{1,0:T(8,128)(2,1)} %get-tuple-element.215), channel_id=1, source_target_pairs={{0,4},{1,5},{2,6},{3,7},{4,0},{5,1},{6,2},{7,3},{8,12},{9,13},{10,... | collective-permute-start | bytes 2359304 | tf_op jit(solution)/shard_map/ppermute | solution.py:895
  378.2 45.3 %collective-permute-start.34 = (bf16[256,1536]{1,0:T(8,128)(2,1)}, bf16[256,1536]{1,0:T(8,128)(2,1)}, u32[]{:S(2)}, u32[]{:S(2)}) collective-permute-start(bf16[256,1536]{1,0:T(8,128)(2,1)} %get-tuple-element.216), channel_id=1, source_target_pairs={{0,2},{1,3},{2,0},{3,1},{4,6},{5,7},{6,4},{7,5},{8,10},{9,11},{10,... | collective-permute-start | bytes 2359304 | tf_op jit(solution)/shard_map/ppermute | solution.py:895
  392.3 36.4 %collective-permute-start.39 = (bf16[48,1536]{1,0:T(8,128)(2,1)S(1)}, bf16[48,1536]{1,0:T(8,128)(2,1)S(1)}, u32[]{:S(2)}, u32[]{:S(2)}) collective-permute-start(bf16[48,1536]{1,0:T(8,128)(2,1)S(1)} %get-tuple-element.223), channel_id=1, source_target_pairs={{0,24},{8,0},{16,8},{24,16},{1,25},{9,1},{17,9},{25,17},{2,26},{10... | collective-permute-start | bytes 442376 | tf_op jit(solution)/shard_map/ppermute | solution.py:932
  395.9 45.3 %collective-permute-start.38 = (bf16[48,1536]{1,0:T(8,128)(2,1)S(1)}, bf16[48,1536]{1,0:T(8,128)(2,1)S(1)}, u32[]{:S(2)}, u32[]{:S(2)}) collective-permute-start(bf16[48,1536]{1,0:T(8,128)(2,1)S(1)} %get-tuple-element.224), channel_id=1, source_target_pairs={{0,16},{8,24},{16,0},{24,8},{1,17},{9,25},{17,1},{25,9},{2,18},{10... | collective-permute-start | bytes 442376 | tf_op jit(solution)/shard_map/ppermute | solution.py:932
  405.4 35.9 %collective-permute-start.37 = (bf16[48,1536]{1,0:T(8,128)(2,1)S(1)}, bf16[48,1536]{1,0:T(8,128)(2,1)S(1)}, u32[]{:S(2)}, u32[]{:S(2)}) collective-permute-start(bf16[48,1536]{1,0:T(8,128)(2,1)S(1)} %get-tuple-element.225), channel_id=1, source_target_pairs={{0,8},{8,16},{16,24},{24,0},{1,9},{9,17},{17,25},{25,1},{2,10},{10... | collective-permute-start | bytes 442376 | tf_op jit(solution)/shard_map/ppermute | solution.py:932
  (53 other events, 587.1 us)
Sparse Core Ops, SparseCore 0:
  12.6 75.0 all-gather.2
  89.5 60.3 all-gather.4
  208.5 35.2 reduce-scatter.4
  245.9 34.2 reduce-scatter.10
  282.4 59.2 reduce-scatter.8
  343.8 86.6 reduce-scatter.6
where the time goes:
time: 463 us; the launch traced here: 459 us
  Pallas kernels  219 us (47%)
  waiting for transfers between devices  109 us (24%)
  starting transfers between devices  48.8 us (11%)
  local copies, waits for them, and re-layouts  35.9 us (8%)
  other arithmetic  31.1 us (7%)
  between operations  14.9 us (3%)
    ppermute x37, waiting for transfers between devices, swap(): return lax.ppermute(values, 'expert', [(i, i ^ bit) for i in range(count)])  84.6 us
    pallas_call x2, Pallas kernels, expert_pass(): call(functools.partial(expert_kernel, e), 'expert_%d' % e, (half,), [spec...  56 us
    ppermute x37, starting transfers between devices, swap(): return lax.ppermute(values, 'expert', [(i, i ^ bit) for i in range(count)])  27.6 us
    pallas_call x1, Pallas kernels, attn_backward(): pl.pallas_call(attn_bwd_kernel, grid_spec=pltpu.PrefetchScalarGridSpec(nu...  26.9 us
    pallas_call x1, Pallas kernels, mix_forward(): call(functools.partial(mix_kernel, count), 'mix', (seq // PAIR,), [spec((...  22.8 us
    pallas_call x2, Pallas kernels, up_grad(): call(up_grad_kernel, 'up_grad', (D // rows,), [spec((seq, rows), lambda s...  22 us
    unnamed x72, local copies, waits for them, and re-layouts  20.8 us
    pallas_call x1, Pallas kernels, attn_forward(): pl.pallas_call(attn_fwd_kernel, grid_spec=pltpu.PrefetchScalarGridSpec(nu...  18.9 us
  transfers between devices with their start and end apart: 50, of which 11 were waited for; matrix products, arithmetic and copies ran while one was open for 12% of the time, Pallas kernels for 41%

commit v1 on v0

--- a/solution.py
+++ b/solution.py
@@ -28,6 +28,21 @@
 BF = jnp.bfloat16
 F32 = jnp.float32
 BOTH = ("dp", "expert")
+
+
+ROOM = {
+    "attn_fwd": 8,
+    "qkv": 24,
+    "back": 12,
+    "pack": 20,
+    "last": 16,
+    "out_grad": 16,
+    "unpack": 12,
+}
+
+
+def room(name):
+    return pltpu.CompilerParams(vmem_limit_bytes=ROOM[name] << 20 if name in ROOM else None)
 
 
 def cost(micros):
@@ -188,6 +203,7 @@
             jax.ShapeDtypeStruct((8, seq), F32),
         ],
         cost_estimate=LONG,
+        compiler_params=room("attn_fwd"),
         name="attn_fwd",
     )(first, q_t, k, v_t, start)
 
@@ -228,6 +244,7 @@
             jax.ShapeDtypeStruct((HEAD_DIM, seq), F32),
         ],
         cost_estimate=cost(20),
+        compiler_params=room("attn_bwd"),
         name="attn_bwd",
     )(first, q_t, da, o_t, lse, k, k_t, v, start)
 
@@ -260,6 +277,7 @@
         ),
         out_shape=out_shape,
         cost_estimate=estimate,
+        compiler_params=room(name),
         name=name,
     )
 
@@ -338,8 +356,24 @@
     )(pos, *pieces, weights, gain, cosine, sine)
 
 
-def send_weights_kernel(groups, members, pos_ref, q_ref, kv_ref, rest_ref, out_ref):
-    query, pair, rest = q_ref[...], kv_ref[...], rest_ref[...]
+def as_column(row):
+    count = row.shape[1]
+    here = lax.broadcasted_iota(jnp.int32, (count, count), 0)
+    there = lax.broadcasted_iota(jnp.int32, (count, count), 1)
+    return jnp.sum(jnp.where(here == there, row.astype(F32), 0.0), axis=1, keepdims=True)
+
+
+def send_weights_kernel(
+    groups, members, pos_ref, q_ref, kv_ref, route_ref, attn_ref, moe_ref, out_ref
+):
+    query, pair = q_ref[...], kv_ref[...]
+    rows, experts = route_ref.shape
+    route = jnp.concatenate(
+        [route_ref[...].astype(F32), jnp.zeros((rows, PACK - QKV - experts), F32)], axis=1
+    )
+    lane = lax.broadcasted_iota(jnp.int32, route.shape, 1)
+    rest = jnp.where(lane == experts, as_column(attn_ref[...]), route)
+    rest = jnp.where(lane == experts + 1, as_column(moe_ref[...]), rest).astype(BF)
     for j in range(members):
         block = jnp.concatenate(
             [query[:, j * Q_COLS : (j + 1) * Q_COLS]]
@@ -351,18 +385,18 @@
             out_ref[i * members + j] = block
 
 
-def send_weights(pos, w_query, w_key_value, rest, groups, members):
-    rows = w_query.shape[0]
+def send_weights(pos, parts, groups, members):
+    rows = parts[0].shape[0]
     full = lambda a: resident(a.shape)
     return call(
         functools.partial(send_weights_kernel, groups, members),
         "send_weights",
         (1,),
-        [full(a) for a in (w_query, w_key_value, rest)],
+        [full(a) for a in parts],
         resident((groups * members, rows, PACK)),
         shape((groups * members, rows, PACK), BF),
         SHORT,
-    )(pos, w_query, w_key_value, rest)
+    )(pos, *parts)
 
 
 def mix_kernel(count, pos_ref, *refs):
@@ -969,16 +1003,9 @@
     first = jnp.stack([start[0, ::BLK] // BLK, (start[0, BLK - 1 :: BLK] + BLK - 1) // BLK])
     x_pieces = gather_pieces(tokens, (start, first))
 
-    rest = jnp.concatenate(
-        [
-            w_router,
-            norm_attn[:, None],
-            norm_moe[:, None],
-            jnp.zeros((in_rows, PACK - QKV - expert_total - 2), BF),
-        ],
-        axis=1,
-    )
-    own = send_weights(pos, w_query, w_key_value, rest, groups, members)
+    own = send_weights(
+        pos, (w_query, w_key_value, w_router, norm_attn[None], norm_moe[None]), groups, members
+    )
     weights = exchange(own, BOTH).reshape(D, PACK)
     gain_attn = weights[:, QKV + expert_total].astype(F32)[None]
     gain_moe = weights[:, QKV + expert_total + 1].astype(F32)[None]

time: 463 us -> 464 us (level)
  Pallas kernels: 219 us -> 193 us
  local copies, waits for them, and re-layouts: 35.9 us -> 48 us
  waiting for transfers between devices: 109 us -> 119 us
  starting transfers between devices: 48.8 us -> 53.7 us
  other arithmetic: 31.1 us -> 26.4 us
    unnamed x72 -> x124, local copies, waits for them, and re-layouts: 20.8 us -> 35.4 us
    pallas_call x1, Pallas kernels: 26.9 us -> 18.5 us  [attn_backward(): pl.pallas_call(attn_bwd_kernel, grid_spec=pltpu.PrefetchScalarGridSpec(nu...]
    ppermute x37, waiting for transfers between devices: 84.6 us -> 91.4 us  [swap(): return lax.ppermute(values, 'expert', [(i, i ^ bit) for i in range(count)])]
    pallas_call x1, Pallas kernels: 18.9 us -> 12.7 us  [attn_forward(): pl.pallas_call(attn_fwd_kernel, grid_spec=pltpu.PrefetchScalarGridSpec(nu...]
    all_to_all x4, starting transfers between devices: 17.3 us -> 22.9 us  [exchange(): return lax.all_to_all(blocks, axes, split_axis=0, concat_axis=0, tiled=True)]
  transfers between devices with their start and end apart: 50 -> 50, of which waited for: 11 -> 13; matrix products, arithmetic and copies ran while one was open for 12% -> 12% of each run, Pallas kernels for 41% -> 35%
where the time goes in v1:
time: 464 us; the launch traced here: 455 us
  Pallas kernels  193 us (42%)
  waiting for transfers between devices  119 us (26%)
  starting transfers between devices  53.7 us (12%)
  local copies, waits for them, and re-layouts  48 us (10%)
  other arithmetic  26.4 us (6%)
  between operations  15.3 us (3%)
    ppermute x37, waiting for transfers between devices, swap(): return lax.ppermute(values, 'expert', [(i, i ^ bit) for i in range(count)])  91.4 us
    pallas_call x2, Pallas kernels, expert_pass(): call(functools.partial(expert_kernel, e), 'expert_%d' % e, (half,), [spec...  56 us
    unnamed x124, local copies, waits for them, and re-layouts  35.4 us
    ppermute x37, starting transfers between devices, swap(): return lax.ppermute(values, 'expert', [(i, i ^ bit) for i in range(count)])  26.3 us
    all_to_all x4, starting transfers between devices, exchange(): return lax.all_to_all(blocks, axes, split_axis=0, concat_axis=0, tiled=True)  22.9 us
    pallas_call x1, Pallas kernels, mix_forward(): call(functools.partial(mix_kernel, count), 'mix', (seq // PAIR,), [spec((...  22.2 us
    pallas_call x2, Pallas kernels, up_grad(): call(up_grad_kernel, 'up_grad', (D // rows,), [spec((seq, rows), lambda s...  22 us
    pallas_call x1, Pallas kernels, attn_backward(): pl.pallas_call(attn_bwd_kernel, grid_spec=pltpu.PrefetchScalarGridSpec(nu...  18.5 us
  transfers between devices with their start and end apart: 50, of which 13 were waited for; matrix products, arithmetic and copies ran while one was open for 12% of the time, Pallas kernels for 35%

profile of v1, /device:TPU:0, one launch (start us, length us, event | category | flops | bytes accessed | tf_op | source)
XLA Modules:
  0.0 455.5 jit_solution(17742095152009111900)
XLA Ops:
  10.8 7.3 %all-to-all-start = ((bf16[32,48,384]{2,1,0:T(8,128)(2,1)}), bf16[32,48,384]{2,1,0:T(8,128)(2,1)S(1)}, u32[]{:S(2)}, u32[]{:S(2)}) async-start(bf16[32,48,384]{2,1,0:T(8,128)(2,1)} %send_weights.1), calls=%async_computation | async-start | bytes 2359296 | tf_op jit(solution)/shard_map/all_to_all | solution.py:971
  23.5 30.2 %collective-permute-done.3.refs_4_ = bf16[256,1536]{1,0:T(8,128)(2,1)S(1)} collective-permute-done((bf16[256,1536]{1,0:T(8,128)(2,1)}, bf16[256,1536]{1,0:T(8,128)(2,1)S(1)}, u32[]{:S(2)}, u32[]{:S(2)}) %collective-permute-start.3) | collective-permute-done | bytes 786464 | tf_op jit(solution)/shard_map/ppermute | solution.py:929
  58.0 6.6 %collective-permute-done.6.refs_7_ = bf16[128,1536]{1,0:T(8,128)(2,1)} collective-permute-done((bf16[128,1536]{1,0:T(8,128)(2,1)S(1)}, bf16[128,1536]{1,0:T(8,128)(2,1)}, u32[]{:S(2)}, u32[]{:S(2)}) %collective-permute-start.6) | collective-permute-done | bytes 393248 | tf_op jit(solution)/shard_map/ppermute | solution.py:929
  69.5 6.9 %qkv.1 = (bf16[192,2048]{1,0:T(8,128)(2,1)S(1)}, bf16[64,2048]{1,0:T(8,128)(2,1)S(1)}, bf16[64,2048]{1,0:T(8,128)(2,1)S(1)}, bf16[2048,64]{1,0:T(8,128)(2,1)S(1)}, bf16[2048,64]{1,0:T(8,128)(2,1)S(1)}) custom-call(s32[1]{0:T(128)} %bitcast.pos_ref, bf16[256,1536]{1,0:T(8,128)(2,1)} %x_ref.1, bf16[256,1536]{1,0:T(8,128)(2,1)} %collective-permute-done.refs_1_, ...), custom_call_target="tpu_custom_call" | custom-call | flops 399999991808 | bytes 10000 | tf_op jit(solution)/shard_map/qkv/pallas_call | solution.py:342
  79.5 12.7 %attn_fwd.1 = (bf16[192,2048]{1,0:T(8,128)(2,1)}, f32[192,2048]{1,0:T(8,128)S(1)}, f32[8,2048]{1,0:T(8,128)S(1)}) custom-call(s32[2,8]{1,0:T(2,128)S(1)} %pad_add_fusion.first_ref, bf16[192,2048]{1,0:T(8,128)(2,1)S(1)} %get-tuple-element.92.q_ref, bf16[2048,64]{1,0:T(8,128)(2,1)S(1)} %get-tuple-element.93.k_ref, ...), custom_call_target="tpu_custom_call" | custom-call | flops 49999998976 | bytes 10000 | tf_op jit(solution)/shard_map/attn_fwd/pallas_call | solution.py:183
  112.8 13.4 %collective-permute-done.19 = s32[8,256]{1,0:T(8,128)S(1)} collective-permute-done((s32[8,256]{1,0:T(8,128)S(1)}, s32[8,256]{1,0:T(8,128)S(1)}, u32[]{:S(2)}, u32[]{:S(2)}) %collective-permute-start.19) | collective-permute-done | bytes 8224 | tf_op jit(solution)/shard_map/ppermute | solution.py:929
  132.6 6.7 %copy.35 = bf16[1536,1536]{0,1:T(8,128)(2,1)} copy(bf16[1536,1536]{1,0:T(8,128)(2,1)} %all-gather.3.cloned.1.call-done) | data formatting | bytes 9437184 | tf_op jit(solution)/shard_map/all_gather | solution.py:1021
  139.2 8.5 %collective-permute-done.15.refs_7_ = bf16[96,2048]{1,0:T(8,128)(2,1)S(1)} collective-permute-done((bf16[96,2048]{1,0:T(8,128)(2,1)}, bf16[96,2048]{1,0:T(8,128)(2,1)S(1)}, u32[]{:S(2)}, u32[]{:S(2)}) %collective-permute-start.15) | collective-permute-done | bytes 393248 | tf_op jit(solution)/shard_map/ppermute | solution.py:929
  153.9 22.2 %mix.1 = (bf16[2048,1536]{1,0:T(8,128)(2,1)}, f32[2048,128]{1,0:T(8,128)}, f32[256,1536]{1,0:T(8,128)}, bf16[256,1536]{1,0:T(8,128)(2,1)}, f32[256,128]{1,0:T(8,128)}) custom-call(s32[1]{0:T(128)} %bitcast.pos_ref, bf16[192,2048]{1,0:T(8,128)(2,1)} %get-tuple-element.95.refs_0_, bf16[192,2048]{1,0:T(8,128)(2,1)} %copy-done.16, bf16[192,2048]{1,0:T(8,128)(2,1)} %copy-done.8, ...), custom_call_target="tpu_custom_call" | custom-call | flops 49999998976 | bytes 10000 | tf_op jit(solution)/shard_map/mix/pallas_call | solution.py:448
  176.1 30.0 %expert_0.1 = (bf16[2048,512]{1,0:T(8,128)(2,1)}, bf16[2048,1024]{1,0:T(8,128)(2,1)}, f32[2048,1536]{1,0:T(8,128)}, f32[8,8,256]{2,1,0:T(8,128)}, bf16[4,512,384]{2,1,0:T(8,128)(2,1)}) custom-call(s32[1]{0:T(128)} %bitcast.pos_ref, bf16[2048,1536]{1,0:T(8,128)(2,1)} %get-tuple-element.125.h2_ref, bf16[2048,1536]{1,0:T(8,128)(2,1)} %all-gather.5.cloned.1.call-done.dy_ref, ...), custom_call_target="tpu_custom_call" | custom-call | flops 5000000000 | bytes 10000 | tf_op jit(solution)/shard_map/expert_0/pallas_call | solution.py:544
  206.2 26.0 %expert_1.1 = (bf16[2048,512]{1,0:T(8,128)(2,1)}, bf16[2048,1024]{1,0:T(8,128)(2,1)}, bf16[4,256,1536]{2,1,0:T(8,128)(2,1)}, bf16[4,256,1536]{2,1,0:T(8,128)(2,1)}, f32[8,8,256]{2,1,0:T(8,128)}) custom-call(s32[1]{0:T(128)} %bitcast.pos_ref, bf16[2048,1536]{1,0:T(8,128)(2,1)} %get-tuple-element.125.h2_ref, ...), custom_call_target="tpu_custom_call" | custom-call | flops 5000000000 | bytes 10000 | tf_op jit(solution)/shard_map/expert_1/pallas_call | solution.py:544
  232.3 7.3 %down_grad.1 = bf16[4,512,384]{2,1,0:T(8,128)(2,1)} custom-call(s32[1]{0:T(128)} %bitcast.pos_ref, bf16[2048,512]{1,0:T(8,128)(2,1)} %get-tuple-element.128.ag_ref.refs_1_, bf16[2048,1536]{1,0:T(8,128)(2,1)} %all-gather.5.cloned.1.call-done.dy_ref), custom_call_target="tpu_custom_call" | custom-call | bytes 10000 | tf_op jit(solution)/shard_map/down_grad/pallas_call | solution.py:580
  249.9 11.1 %up_grad.2 = bf16[1536,1024]{1,0:T(8,128)(2,1)} custom-call(s32[1]{0:T(128)} %bitcast.pos_ref, bf16[2048,1536]{1,0:T(8,128)(2,1)} %get-tuple-element.125.h2_ref, bf16[2048,1024]{1,0:T(8,128)(2,1)} %get-tuple-element.124.dgu_ref), custom_call_target="tpu_custom_call" | custom-call | bytes 10000 | tf_op jit(solution)/shard_map/up_grad/pallas_call | solution.py:599
  261.1 10.9 %up_grad.3 = bf16[1536,1024]{1,0:T(8,128)(2,1)} custom-call(s32[1]{0:T(128)} %bitcast.pos_ref, bf16[2048,1536]{1,0:T(8,128)(2,1)} %get-tuple-element.125.h2_ref, bf16[2048,1024]{1,0:T(8,128)(2,1)} %get-tuple-element.126.dgu_ref), custom_call_target="tpu_custom_call" | custom-call | bytes 10000 | tf_op jit(solution)/shard_map/up_grad/pallas_call | solution.py:599
  272.0 10.5 %combine.1 = (bf16[4,256,1536]{2,1,0:T(8,128)(2,1)}, bf16[4,256,1536]{2,1,0:T(8,128)(2,1)}) custom-call(s32[1]{0:T(128)} %bitcast.pos_ref, bf16[2048,512]{1,0:T(8,128)(2,1)} %get-tuple-element.127.refs_0_, bf16[2048,512]{1,0:T(8,128)(2,1)} %get-tuple-element.128.ag_ref.refs_1_, bf16[2,512,1536]{2,1,0:T(8,128)(2,1)} %refs_2_.1), custom_call_target="tpu_custom_call" | custom-call | bytes 10000 | tf_op jit(solution)/shard_map/combine/pallas_call | solution.py:624
  285.2 9.0 %middle.1 = (f32[256,1536]{1,0:T(8,128)}, bf16[256,1536]{1,0:T(8,128)(2,1)}, bf16[8,384,256]{2,1,0:T(8,128)(2,1)}, f32[1536,128]{1,0:T(8,128)}, f32[8,1536]{1,0:T(8,128)}) custom-call(s32[1]{0:T(128)} %bitcast.pos_ref, bf16[4,256,1536]{2,1,0:T(8,128)(2,1)} %get-tuple-element.133.keep_ref, bf16[4,256,1536]{2,1,0:T(8,128)(2,1)} %collective-permute-done.25.got_ref, ...), custom_call_target="tpu_custom_call" | custom-call | flops 99999997952 | bytes 10000 | tf_op jit(solution)/shard_map/middle/pallas_call | solution.py:684
  308.7 11.2 %all-to-all-done.2.da_ref.refs_10_ = bf16[8,384,256]{2,1,0:T(8,128)(2,1)S(1)} async-done(((bf16[8,384,256]{2,1,0:T(8,128)(2,1)}), bf16[8,384,256]{2,1,0:T(8,128)(2,1)S(1)}, u32[]{:S(2)}, u32[]{:S(2)}) %all-to-all-start.2) | async-done | bytes 1572896 | tf_op jit(solution)/shard_map/all_to_all | solution.py:971
  321.1 18.5 %attn_bwd.1 = (f32[192,2048]{1,0:T(8,128)}, f32[64,2048]{1,0:T(8,128)}, f32[64,2048]{1,0:T(8,128)}) custom-call(s32[2,8]{1,0:T(2,128)} %copy-done.30, bf16[192,2048]{1,0:T(8,128)(2,1)} %copy-done.34, bf16[8,384,256]{2,1,0:T(8,128)(2,1)} %copy-done.2, f32[192,2048]{1,0:T(8,128)} %copy-done.33, f32[8,2048]{1,0:T(8,128)} %copy-done.40, ...), custom_call_target="tpu_custom_call" | custom-call | flops 20000000000 | bytes 10000 | tf_op jit(solution)/shard_map/attn_bwd/pallas_call | solution.py:216
  350.4 8.5 %pack.1 = bf16[1536,384]{1,0:T(8,128)(2,1)S(1)} custom-call(s32[1]{0:T(128)} %bitcast.pos_ref, bf16[384,2048]{1,0:T(8,128)(2,1)S(1)} %get-tuple-element.151.packed_ref, bf16[8,256,1536]{2,1,0:T(8,128)(2,1)} %bitcast.9.refs_10_.x_ref, f32[1,1536]{1,0:T(1,128)S(1)} %copy-done.29, bf16[1536,384]{1,0:T(8,128)(2,1)S(1)} %bitcast.61, f32[1536,128]{1,0:T(8,128)S(1)} %copy-done.39, ...), custom_call_target="tpu_custom_call" | custom-call | flops 49999998976 | bytes 10000 | tf_op jit(solution)/shard_map/pack/pallas_call | solution.py:805
  359.9 8.2 %all-to-all-start.3 = ((bf16[32,48,384]{2,1,0:T(8,128)(2,1)}), bf16[32,48,384]{2,1,0:T(8,128)(2,1)S(1)}, u32[]{:S(2)}, u32[]{:S(2)}) async-start(bf16[32,48,384]{2,1,0:T(8,128)(2,1)} %bitcast.62), calls=%async_computation.4 | async-start | bytes 2359296 | tf_op jit(solution)/shard_map/all_to_all | solution.py:971
  378.8 7.0 %out_grad.1 = f32[192,1536]{1,0:T(8,128)S(1)} custom-call(s32[1]{0:T(128)} %bitcast.pos_ref, bf16[192,2048]{1,0:T(8,128)(2,1)} %get-tuple-element.95.refs_0_, bf16[192,2048]{1,0:T(8,128)(2,1)S(1)} %copy-done.17, bf16[192,2048]{1,0:T(8,128)(2,1)S(1)} %copy-done.9, bf16[192,2048]{1,0:T(8,128)(2,1)} %collective-permute-done.11.refs_3_, ...), custom_call_target="tpu_custom_call" | custom-call | bytes 10000 | tf_op jit(solution)/shard_map/out_grad/pallas_call | solution.py:881
  389.8 11.2 %collective-permute-done.36.fd_ref = bf16[256,1536]{1,0:T(8,128)(2,1)S(1)} collective-permute-done((bf16[256,1536]{1,0:T(8,128)(2,1)S(1)}, bf16[256,1536]{1,0:T(8,128)(2,1)S(1)}, u32[]{:S(2)}, u32[]{:S(2)}) %collective-permute-start.36) | collective-permute-done | bytes 786464 | tf_op jit(solution)/shard_map/ppermute | solution.py:929
  401.4 16.4 %collective-permute-done.35.fy_ref = bf16[256,1536]{1,0:T(8,128)(2,1)S(1)} collective-permute-done((bf16[256,1536]{1,0:T(8,128)(2,1)S(1)}, bf16[256,1536]{1,0:T(8,128)(2,1)S(1)}, u32[]{:S(2)}, u32[]{:S(2)}) %collective-permute-start.35) | collective-permute-done | bytes 786464 | tf_op jit(solution)/shard_map/ppermute | solution.py:929
  423.5 15.9 %collective-permute-done.38 = bf16[48,1536]{1,0:T(8,128)(2,1)S(1)} collective-permute-done((bf16[48,1536]{1,0:T(8,128)(2,1)S(1)}, bf16[48,1536]{1,0:T(8,128)(2,1)S(1)}, u32[]{:S(2)}, u32[]{:S(2)}) %collective-permute-start.38) | collective-permute-done | bytes 147488 | tf_op jit(solution)/shard_map/ppermute | solution.py:966
  (256 shorter events, 123.8 us)
Async XLA Ops:
  7.2 125.4 %all-gather.3.cloned.1.call-start = ((), (), s32[]{:S(2)}) async-start(), calls=%async_computation.8 | async-start | bytes 4866048 | tf_op jit(solution)/shard_map/all_gather | solution.py:1021
  10.8 56.9 %all-to-all-start = ((bf16[32,48,384]{2,1,0:T(8,128)(2,1)}), bf16[32,48,384]{2,1,0:T(8,128)(2,1)S(1)}, u32[]{:S(2)}, u32[]{:S(2)}) async-start(bf16[32,48,384]{2,1,0:T(8,128)(2,1)} %send_weights.1), calls=%async_computation | async-start | bytes 2359296 | tf_op jit(solution)/shard_map/all_to_all | solution.py:971
  18.1 158.0 %all-gather.5.cloned.1.call-start = ((), (), s32[]{:S(2)}) async-start(), calls=%async_computation.9 | async-start | bytes 7077888 | tf_op jit(solution)/shard_map/all_gather | solution.py:1022
  20.0 35.7 %collective-permute-start.1 = (bf16[256,1536]{1,0:T(8,128)(2,1)}, bf16[256,1536]{1,0:T(8,128)(2,1)S(1)}, u32[]{:S(2)}, u32[]{:S(2)}) collective-permute-start(bf16[256,1536]{1,0:T(8,128)(2,1)} %x_ref.1), channel_id=1, source_target_pairs={{0,2},{1,3},{2,0},{3,1},{4,6},{5,7},{6,4},{7,5},{8,10},{9,11},{10,... | collective-permute-start | bytes 2359304 | tf_op jit(solution)/shard_map/ppermute | solution.py:929
  21.5 47.4 %collective-permute-start = (bf16[256,1536]{1,0:T(8,128)(2,1)}, bf16[256,1536]{1,0:T(8,128)(2,1)}, u32[]{:S(2)}, u32[]{:S(2)}) collective-permute-start(bf16[256,1536]{1,0:T(8,128)(2,1)} %x_ref.1), channel_id=1, source_target_pairs={{0,1},{1,0},{2,3},{3,2},{4,5},{5,4},{6,7},{7,6},{8,9},{9,8},{10,11... | collective-permute-start | bytes 2359304 | tf_op jit(solution)/shard_map/ppermute | solution.py:929
  21.5 228.4 %reduce-scatter.5.cloned.1.call-start = ((), (), s32[]{:S(2)}) async-start(), calls=%async_computation.10 | async-start | bytes 1966080 | tf_op jit(solution)/shard_map/reduce_scatter | solution.py:1049
  76.5 35.8 %collective-permute-start.21 = (s32[8,256]{1,0:T(8,128)S(1)}, s32[8,256]{1,0:T(8,128)S(1)}, u32[]{:S(2)}, u32[]{:S(2)}) collective-permute-start(s32[8,256]{1,0:T(8,128)S(1)} %bitcast.78), channel_id=1, source_target_pairs={{0,6},{1,7},{2,4},{3,5},{4,2},{5,3},{6,0},{7,1},{8,14},{9,15},{10,... | collective-permute-start | bytes 24584 | tf_op jit(solution)/shard_map/ppermute | solution.py:929
  112.3 39.9 %collective-permute-start.9 = (bf16[192,2048]{1,0:T(8,128)(2,1)}, bf16[192,2048]{1,0:T(8,128)(2,1)S(1)}, u32[]{:S(2)}, u32[]{:S(2)}) collective-permute-start(bf16[192,2048]{1,0:T(8,128)(2,1)} %get-tuple-element.95.refs_0_), channel_id=1, source_target_pairs={{0,1},{1,0},{2,3},{3,2},{4,5},{5,4},{6,7},{7,6},{8,9},{9,8},{10,11... | collective-permute-start | bytes 2359304 | tf_op jit(solution)/shard_map/ppermute | solution.py:929
  206.2 92.7 %reduce-scatter.11.cloned.1.call-start = ((), (), s32[]{:S(2)}) async-start(), calls=%async_computation.13 | async-start | bytes 1966080 | tf_op jit(solution)/shard_map/reduce_scatter | solution.py:1049
  243.0 40.8 %collective-permute-start.29 = (bf16[256,1536]{1,0:T(8,128)(2,1)}, bf16[256,1536]{1,0:T(8,128)(2,1)S(1)}, u32[]{:S(2)}, u32[]{:S(2)}) collective-permute-start(bf16[256,1536]{1,0:T(8,128)(2,1)} %get-tuple-element.220), channel_id=1, source_target_pairs={{0,6},{1,7},{2,4},{3,5},{4,2},{5,3},{6,0},{7,1},{8,14},{9,15},{10,... | collective-permute-start | bytes 2359304 | tf_op jit(solution)/shard_map/ppermute | solution.py:929
  243.6 40.2 %collective-permute-start.28 = (bf16[256,1536]{1,0:T(8,128)(2,1)}, bf16[256,1536]{1,0:T(8,128)(2,1)S(1)}, u32[]{:S(2)}, u32[]{:S(2)}) collective-permute-start(bf16[256,1536]{1,0:T(8,128)(2,1)} %get-tuple-element.221), channel_id=1, source_target_pairs={{0,4},{1,5},{2,6},{3,7},{4,0},{5,1},{6,2},{7,3},{8,12},{9,13},{10,... | collective-permute-start | bytes 2359304 | tf_op jit(solution)/shard_map/ppermute | solution.py:929
  244.5 39.3 %collective-permute-start.27 = (bf16[256,1536]{1,0:T(8,128)(2,1)}, bf16[256,1536]{1,0:T(8,128)(2,1)S(1)}, u32[]{:S(2)}, u32[]{:S(2)}) collective-permute-start(bf16[256,1536]{1,0:T(8,128)(2,1)} %get-tuple-element.222), channel_id=1, source_target_pairs={{0,2},{1,3},{2,0},{3,1},{4,6},{5,7},{6,4},{7,5},{8,10},{9,11},{10,... | collective-permute-start | bytes 2359304 | tf_op jit(solution)/shard_map/ppermute | solution.py:929
  246.5 36.4 %all-to-all-start.1 = ((f32[8,8,256]{2,1,0:T(8,128)}), f32[8,8,256]{2,1,0:T(8,128)S(1)}, u32[]{:S(2)}, u32[]{:S(2)}) async-start(f32[8,8,256]{2,1,0:T(8,128)} %get-tuple-element.137), calls=%async_computation.2 | async-start | bytes 131072 | tf_op jit(solution)/shard_map/all_to_all | solution.py:971
  249.9 194.4 %reduce-scatter.9.cloned.1.call-start = ((), (), s32[]{:S(2)}) async-start(), calls=%async_computation.12 | async-start | bytes 3932160 | tf_op jit(solution)/shard_map/reduce_scatter | solution.py:1050
  298.3 146.0 %reduce-scatter.7.cloned.1.call-start = ((), (), s32[]{:S(2)}) async-start(), calls=%async_computation.11 | async-start | bytes 3932160 | tf_op jit(solution)/shard_map/reduce_scatter | solution.py:1050
  305.2 69.2 %collective-permute-start.32 = (bf16[256,1536]{1,0:T(8,128)(2,1)}, bf16[256,1536]{1,0:T(8,128)(2,1)}, u32[]{:S(2)}, u32[]{:S(2)}) collective-permute-start(bf16[256,1536]{1,0:T(8,128)(2,1)} %get-tuple-element.217), channel_id=1, source_target_pairs={{0,6},{1,7},{2,4},{3,5},{4,2},{5,3},{6,0},{7,1},{8,14},{9,15},{10,... | collective-permute-start | bytes 2359304 | tf_op jit(solution)/shard_map/ppermute | solution.py:929
  308.1 66.8 %collective-permute-start.31 = (bf16[256,1536]{1,0:T(8,128)(2,1)}, bf16[256,1536]{1,0:T(8,128)(2,1)}, u32[]{:S(2)}, u32[]{:S(2)}) collective-permute-start(bf16[256,1536]{1,0:T(8,128)(2,1)} %get-tuple-element.218), channel_id=1, source_target_pairs={{0,4},{1,5},{2,6},{3,7},{4,0},{5,1},{6,2},{7,3},{8,12},{9,13},{10,... | collective-permute-start | bytes 2359304 | tf_op jit(solution)/shard_map/ppermute | solution.py:929
  308.7 66.2 %collective-permute-start.30 = (bf16[256,1536]{1,0:T(8,128)(2,1)}, bf16[256,1536]{1,0:T(8,128)(2,1)}, u32[]{:S(2)}, u32[]{:S(2)}) collective-permute-start(bf16[256,1536]{1,0:T(8,128)(2,1)} %get-tuple-element.219), channel_id=1, source_target_pairs={{0,2},{1,3},{2,0},{3,1},{4,6},{5,7},{6,4},{7,5},{8,10},{9,11},{10,... | collective-permute-start | bytes 2359304 | tf_op jit(solution)/shard_map/ppermute | solution.py:929
  359.9 80.8 %all-to-all-start.3 = ((bf16[32,48,384]{2,1,0:T(8,128)(2,1)}), bf16[32,48,384]{2,1,0:T(8,128)(2,1)S(1)}, u32[]{:S(2)}, u32[]{:S(2)}) async-start(bf16[32,48,384]{2,1,0:T(8,128)(2,1)} %bitcast.62), calls=%async_computation.4 | async-start | bytes 2359296 | tf_op jit(solution)/shard_map/all_to_all | solution.py:971
  373.9 43.9 %collective-permute-start.35 = (bf16[256,1536]{1,0:T(8,128)(2,1)S(1)}, bf16[256,1536]{1,0:T(8,128)(2,1)S(1)}, u32[]{:S(2)}, u32[]{:S(2)}) collective-permute-start(bf16[256,1536]{1,0:T(8,128)(2,1)S(1)} %get-tuple-element.215), channel_id=1, source_target_pairs={{0,4},{1,5},{2,6},{3,7},{4,0},{5,1},{6,2},{7,3},{8,12},{9,13},{10,... | collective-permute-start | bytes 2359304 | tf_op jit(solution)/shard_map/ppermute | solution.py:929
  374.5 45.3 %collective-permute-start.34 = (bf16[256,1536]{1,0:T(8,128)(2,1)S(1)}, bf16[256,1536]{1,0:T(8,128)(2,1)S(1)}, u32[]{:S(2)}, u32[]{:S(2)}) collective-permute-start(bf16[256,1536]{1,0:T(8,128)(2,1)S(1)} %get-tuple-element.216), channel_id=1, source_target_pairs={{0,2},{1,3},{2,0},{3,1},{4,6},{5,7},{6,4},{7,5},{8,10},{9,11},{10,... | collective-permute-start | bytes 2359304 | tf_op jit(solution)/shard_map/ppermute | solution.py:929
  386.0 37.5 %collective-permute-start.39 = (bf16[48,1536]{1,0:T(8,128)(2,1)S(1)}, bf16[48,1536]{1,0:T(8,128)(2,1)S(1)}, u32[]{:S(2)}, u32[]{:S(2)}) collective-permute-start(bf16[48,1536]{1,0:T(8,128)(2,1)S(1)} %get-tuple-element.223), channel_id=1, source_target_pairs={{0,24},{8,0},{16,8},{24,16},{1,25},{9,1},{17,9},{25,17},{2,26},{10... | collective-permute-start | bytes 442376 | tf_op jit(solution)/shard_map/ppermute | solution.py:966
  389.8 49.7 %collective-permute-start.38 = (bf16[48,1536]{1,0:T(8,128)(2,1)S(1)}, bf16[48,1536]{1,0:T(8,128)(2,1)S(1)}, u32[]{:S(2)}, u32[]{:S(2)}) collective-permute-start(bf16[48,1536]{1,0:T(8,128)(2,1)S(1)} %get-tuple-element.224), channel_id=1, source_target_pairs={{0,16},{8,24},{16,0},{24,8},{1,17},{9,25},{17,1},{25,9},{2,18},{10... | collective-permute-start | bytes 442376 | tf_op jit(solution)/shard_map/ppermute | solution.py:966
  401.0 38.5 %collective-permute-start.37 = (bf16[48,1536]{1,0:T(8,128)(2,1)S(1)}, bf16[48,1536]{1,0:T(8,128)(2,1)S(1)}, u32[]{:S(2)}, u32[]{:S(2)}) collective-permute-start(bf16[48,1536]{1,0:T(8,128)(2,1)S(1)} %get-tuple-element.225), channel_id=1, source_target_pairs={{0,8},{8,16},{16,24},{24,0},{1,9},{9,17},{17,25},{25,1},{2,10},{10... | collective-permute-start | bytes 442376 | tf_op jit(solution)/shard_map/ppermute | solution.py:966
  (79 other events, 953.9 us)
Sparse Core Ops, SparseCore 0:
  10.9 75.0 all-gather.2
  87.9 61.0 all-gather.4
  206.3 35.6 reduce-scatter.4
  244.1 34.2 reduce-scatter.10
  280.6 59.2 reduce-scatter.8
  342.0 87.6 reduce-scatter.6

commit v2 on v1

--- a/solution.py
+++ b/solution.py
@@ -1073,7 +1073,8 @@
     out_terms = send_to_groups(out_wgrad)
     came = exchange(sent.reshape(devices, in_rows, PACK), BOTH)
     token_grad = last(pos, keep1, got1, came_sums1, tokens, gain_attn, dy1)
-    query_share, pair_share, rest = unpack(pos, tie(came, token_grad), groups)
+    up_share = jnp.stack(tie(up_share, token_grad)).astype(F32)
+    query_share, pair_share, rest = unpack(pos, tie(came, up_share), groups)
     router_share = (
         rest[:, ROUTE : ROUTE + expert_total]
         + rest[:, ROUTE + expert_total : ROUTE + 2 * expert_total]
@@ -1081,7 +1082,7 @@
     moe_gain_share = rest[:, ROUTE + 32] + rest[:, ROUTE + 33]
 
     attn_gain_share = rest[:, ROUTE + 34] + rest[:, ROUTE + 35]
-    out_share = sum(term.astype(F32) for term in tie(out_terms, token_grad)).T
+    out_share = sum(term.astype(F32) for term in tie(out_terms, up_share)).T
 
     return (
         result,
@@ -1092,7 +1093,7 @@
         router_share,
         attn_gain_share,
         moe_gain_share,
-        jnp.stack(tie(up_share, rest, out_share)).astype(F32),
+        up_share,
         jnp.stack(down_share).astype(F32),
     )
 

time: 464 us -> 457 us (0.985)
  waiting for transfers between devices: 119 us -> 107 us
  Pallas kernels: 193 us -> 203 us
    ppermute x3, waiting for transfers between devices: 15.9 us -> 5.38 us  [send_to_groups(): lax.ppermute(sent, 'dp', [(i, (i + k) % count) for i in range(count)])]
    pallas_call x1, Pallas kernels: 18.5 us -> 24.3 us  [attn_backward(): pl.pallas_call(attn_bwd_kernel, grid_spec=pltpu.PrefetchScalarGridSpec(nu...]
    all_to_all x4, starting transfers between devices: 22.9 us -> 17.4 us  [exchange(): return lax.all_to_all(blocks, axes, split_axis=0, concat_axis=0, tiled=True)]
    ppermute x37, waiting for transfers between devices: 91.4 us -> 86 us  [swap(): return lax.ppermute(values, 'expert', [(i, i ^ bit) for i in range(count)])]
    unnamed x124 -> x120, local copies, waits for them, and re-layouts: 35.4 us -> 34.4 us
  transfers between devices with their start and end apart: 50 -> 50, of which waited for: 13 -> 15; matrix products, arithmetic and copies ran while one was open for 12% -> 13% of each run, Pallas kernels for 35% -> 38%
where the time goes in v2:
time: 457 us; the launch traced here: 448 us
  Pallas kernels  203 us (44%)
  waiting for transfers between devices  107 us (23%)
  starting transfers between devices  49.5 us (11%)
  local copies, waits for them, and re-layouts  47 us (10%)
  other arithmetic  26.4 us (6%)
  between operations  15.3 us (3%)
    ppermute x37, waiting for transfers between devices, swap(): return lax.ppermute(values, 'expert', [(i, i ^ bit) for i in range(count)])  86 us
    pallas_call x2, Pallas kernels, expert_pass(): call(functools.partial(expert_kernel, e), 'expert_%d' % e, (half,), [spec...  56.3 us
    unnamed x120, local copies, waits for them, and re-layouts  34.4 us
    ppermute x37, starting transfers between devices, swap(): return lax.ppermute(values, 'expert', [(i, i ^ bit) for i in range(count)])  27.7 us
    pallas_call x1, Pallas kernels, attn_backward(): pl.pallas_call(attn_bwd_kernel, grid_spec=pltpu.PrefetchScalarGridSpec(nu...  24.3 us
    pallas_call x1, Pallas kernels, mix_forward(): call(functools.partial(mix_kernel, count), 'mix', (seq // PAIR,), [spec((...  22.2 us
    pallas_call x2, Pallas kernels, up_grad(): call(up_grad_kernel, 'up_grad', (D // rows,), [spec((seq, rows), lambda s...  22 us
    all_to_all x4, starting transfers between devices, exchange(): return lax.all_to_all(blocks, axes, split_axis=0, concat_axis=0, tiled=True)  17.4 us
  transfers between devices with their start and end apart: 50, of which 15 were waited for; matrix products, arithmetic and copies ran while one was open for 13% of the time, Pallas kernels for 38%

profile of v2, /device:TPU:0, one launch (start us, length us, event | category | flops | bytes accessed | tf_op | source)
XLA Modules:
  0.0 448.4 jit_solution(8329762511717580374)
XLA Ops:
  10.8 7.3 %all-to-all-start = ((bf16[32,48,384]{2,1,0:T(8,128)(2,1)}), bf16[32,48,384]{2,1,0:T(8,128)(2,1)S(1)}, u32[]{:S(2)}, u32[]{:S(2)}) async-start(bf16[32,48,384]{2,1,0:T(8,128)(2,1)} %send_weights.1), calls=%async_computation | async-start | bytes 2359296 | tf_op jit(solution)/shard_map/all_to_all | solution.py:971
  23.5 30.2 %collective-permute-done.3.refs_4_ = bf16[256,1536]{1,0:T(8,128)(2,1)S(1)} collective-permute-done((bf16[256,1536]{1,0:T(8,128)(2,1)}, bf16[256,1536]{1,0:T(8,128)(2,1)S(1)}, u32[]{:S(2)}, u32[]{:S(2)}) %collective-permute-start.3) | collective-permute-done | bytes 786464 | tf_op jit(solution)/shard_map/ppermute | solution.py:929
  58.0 6.6 %collective-permute-done.6.refs_7_ = bf16[128,1536]{1,0:T(8,128)(2,1)} collective-permute-done((bf16[128,1536]{1,0:T(8,128)(2,1)S(1)}, bf16[128,1536]{1,0:T(8,128)(2,1)}, u32[]{:S(2)}, u32[]{:S(2)}) %collective-permute-start.6) | collective-permute-done | bytes 393248 | tf_op jit(solution)/shard_map/ppermute | solution.py:929
  69.5 6.9 %qkv.1 = (bf16[192,2048]{1,0:T(8,128)(2,1)S(1)}, bf16[64,2048]{1,0:T(8,128)(2,1)S(1)}, bf16[64,2048]{1,0:T(8,128)(2,1)S(1)}, bf16[2048,64]{1,0:T(8,128)(2,1)S(1)}, bf16[2048,64]{1,0:T(8,128)(2,1)S(1)}) custom-call(s32[1]{0:T(128)} %bitcast.pos_ref, bf16[256,1536]{1,0:T(8,128)(2,1)} %x_ref.1, bf16[256,1536]{1,0:T(8,128)(2,1)} %collective-permute-done.refs_1_, ...), custom_call_target="tpu_custom_call" | custom-call | flops 399999991808 | bytes 10000 | tf_op jit(solution)/shard_map/qkv/pallas_call | solution.py:342
  79.5 16.8 %attn_fwd.1 = (bf16[192,2048]{1,0:T(8,128)(2,1)}, f32[192,2048]{1,0:T(8,128)S(1)}, f32[8,2048]{1,0:T(8,128)S(1)}) custom-call(s32[2,8]{1,0:T(2,128)S(1)} %pad_add_fusion.first_ref, bf16[192,2048]{1,0:T(8,128)(2,1)S(1)} %get-tuple-element.92.q_ref, bf16[2048,64]{1,0:T(8,128)(2,1)S(1)} %get-tuple-element.93.k_ref, ...), custom_call_target="tpu_custom_call" | custom-call | flops 49999998976 | bytes 10000 | tf_op jit(solution)/shard_map/attn_fwd/pallas_call | solution.py:183
  116.8 7.2 %collective-permute-done.19 = s32[8,256]{1,0:T(8,128)S(1)} collective-permute-done((s32[8,256]{1,0:T(8,128)S(1)}, s32[8,256]{1,0:T(8,128)S(1)}, u32[]{:S(2)}, u32[]{:S(2)}) %collective-permute-start.19) | collective-permute-done | bytes 8224 | tf_op jit(solution)/shard_map/ppermute | solution.py:929
  131.9 6.7 %copy.35 = bf16[1536,1536]{0,1:T(8,128)(2,1)} copy(bf16[1536,1536]{1,0:T(8,128)(2,1)} %all-gather.3.cloned.1.call-done) | data formatting | bytes 9437184 | tf_op jit(solution)/shard_map/all_gather | solution.py:1021
  138.7 7.6 %collective-permute-done.15.refs_7_ = bf16[96,2048]{1,0:T(8,128)(2,1)S(1)} collective-permute-done((bf16[96,2048]{1,0:T(8,128)(2,1)}, bf16[96,2048]{1,0:T(8,128)(2,1)S(1)}, u32[]{:S(2)}, u32[]{:S(2)}) %collective-permute-start.15) | collective-permute-done | bytes 393248 | tf_op jit(solution)/shard_map/ppermute | solution.py:929
  154.2 22.2 %mix.1 = (bf16[2048,1536]{1,0:T(8,128)(2,1)}, f32[2048,128]{1,0:T(8,128)}, f32[256,1536]{1,0:T(8,128)}, bf16[256,1536]{1,0:T(8,128)(2,1)}, f32[256,128]{1,0:T(8,128)}) custom-call(s32[1]{0:T(128)} %bitcast.pos_ref, bf16[192,2048]{1,0:T(8,128)(2,1)} %get-tuple-element.95.refs_0_, bf16[192,2048]{1,0:T(8,128)(2,1)} %copy-done.16, bf16[192,2048]{1,0:T(8,128)(2,1)} %copy-done.8, ...), custom_call_target="tpu_custom_call" | custom-call | flops 49999998976 | bytes 10000 | tf_op jit(solution)/shard_map/mix/pallas_call | solution.py:448
  176.5 30.0 %expert_0.1 = (bf16[2048,512]{1,0:T(8,128)(2,1)}, bf16[2048,1024]{1,0:T(8,128)(2,1)}, f32[2048,1536]{1,0:T(8,128)}, f32[8,8,256]{2,1,0:T(8,128)}, bf16[4,512,384]{2,1,0:T(8,128)(2,1)}) custom-call(s32[1]{0:T(128)} %bitcast.pos_ref, bf16[2048,1536]{1,0:T(8,128)(2,1)} %get-tuple-element.125.h2_ref, bf16[2048,1536]{1,0:T(8,128)(2,1)} %all-gather.5.cloned.1.call-done.dy_ref, ...), custom_call_target="tpu_custom_call" | custom-call | flops 5000000000 | bytes 10000 | tf_op jit(solution)/shard_map/expert_0/pallas_call | solution.py:544
  206.6 26.3 %expert_1.1 = (bf16[2048,512]{1,0:T(8,128)(2,1)}, bf16[2048,1024]{1,0:T(8,128)(2,1)}, bf16[4,256,1536]{2,1,0:T(8,128)(2,1)}, bf16[4,256,1536]{2,1,0:T(8,128)(2,1)}, f32[8,8,256]{2,1,0:T(8,128)}) custom-call(s32[1]{0:T(128)} %bitcast.pos_ref, bf16[2048,1536]{1,0:T(8,128)(2,1)} %get-tuple-element.125.h2_ref, ...), custom_call_target="tpu_custom_call" | custom-call | flops 5000000000 | bytes 10000 | tf_op jit(solution)/shard_map/expert_1/pallas_call | solution.py:544
  233.0 7.3 %down_grad.1 = bf16[4,512,384]{2,1,0:T(8,128)(2,1)} custom-call(s32[1]{0:T(128)} %bitcast.pos_ref, bf16[2048,512]{1,0:T(8,128)(2,1)} %get-tuple-element.128.ag_ref.refs_1_, bf16[2048,1536]{1,0:T(8,128)(2,1)} %all-gather.5.cloned.1.call-done.dy_ref), custom_call_target="tpu_custom_call" | custom-call | bytes 10000 | tf_op jit(solution)/shard_map/down_grad/pallas_call | solution.py:580
  250.6 11.1 %up_grad.2 = bf16[1536,1024]{1,0:T(8,128)(2,1)} custom-call(s32[1]{0:T(128)} %bitcast.pos_ref, bf16[2048,1536]{1,0:T(8,128)(2,1)} %get-tuple-element.125.h2_ref, bf16[2048,1024]{1,0:T(8,128)(2,1)} %get-tuple-element.124.dgu_ref), custom_call_target="tpu_custom_call" | custom-call | bytes 10000 | tf_op jit(solution)/shard_map/up_grad/pallas_call | solution.py:599
  261.7 10.9 %up_grad.3 = bf16[1536,1024]{1,0:T(8,128)(2,1)} custom-call(s32[1]{0:T(128)} %bitcast.pos_ref, bf16[2048,1536]{1,0:T(8,128)(2,1)} %get-tuple-element.125.h2_ref, bf16[2048,1024]{1,0:T(8,128)(2,1)} %get-tuple-element.126.dgu_ref), custom_call_target="tpu_custom_call" | custom-call | bytes 10000 | tf_op jit(solution)/shard_map/up_grad/pallas_call | solution.py:599
  272.7 10.6 %combine.1 = (bf16[4,256,1536]{2,1,0:T(8,128)(2,1)}, bf16[4,256,1536]{2,1,0:T(8,128)(2,1)}) custom-call(s32[1]{0:T(128)} %bitcast.pos_ref, bf16[2048,512]{1,0:T(8,128)(2,1)} %get-tuple-element.127.refs_0_, bf16[2048,512]{1,0:T(8,128)(2,1)} %get-tuple-element.128.ag_ref.refs_1_, bf16[2,512,1536]{2,1,0:T(8,128)(2,1)} %refs_2_.1), custom_call_target="tpu_custom_call" | custom-call | bytes 10000 | tf_op jit(solution)/shard_map/combine/pallas_call | solution.py:624
  285.8 8.7 %middle.1 = (f32[256,1536]{1,0:T(8,128)}, bf16[256,1536]{1,0:T(8,128)(2,1)}, bf16[8,384,256]{2,1,0:T(8,128)(2,1)}, f32[1536,128]{1,0:T(8,128)}, f32[8,1536]{1,0:T(8,128)}) custom-call(s32[1]{0:T(128)} %bitcast.pos_ref, bf16[4,256,1536]{2,1,0:T(8,128)(2,1)} %get-tuple-element.133.keep_ref, bf16[4,256,1536]{2,1,0:T(8,128)(2,1)} %collective-permute-done.25.got_ref, ...), custom_call_target="tpu_custom_call" | custom-call | flops 99999997952 | bytes 10000 | tf_op jit(solution)/shard_map/middle/pallas_call | solution.py:684
  309.0 11.2 %all-to-all-done.2.da_ref.refs_10_ = bf16[8,384,256]{2,1,0:T(8,128)(2,1)S(1)} async-done(((bf16[8,384,256]{2,1,0:T(8,128)(2,1)}), bf16[8,384,256]{2,1,0:T(8,128)(2,1)S(1)}, u32[]{:S(2)}, u32[]{:S(2)}) %all-to-all-start.2) | async-done | bytes 1572896 | tf_op jit(solution)/shard_map/all_to_all | solution.py:971
  321.4 24.3 %attn_bwd.1 = (f32[192,2048]{1,0:T(8,128)}, f32[64,2048]{1,0:T(8,128)}, f32[64,2048]{1,0:T(8,128)}) custom-call(s32[2,8]{1,0:T(2,128)} %copy-done.30, bf16[192,2048]{1,0:T(8,128)(2,1)} %copy-done.34, bf16[8,384,256]{2,1,0:T(8,128)(2,1)} %copy-done.2, f32[192,2048]{1,0:T(8,128)} %copy-done.33, f32[8,2048]{1,0:T(8,128)} %copy-done.40, ...), custom_call_target="tpu_custom_call" | custom-call | flops 20000000000 | bytes 10000 | tf_op jit(solution)/shard_map/attn_bwd/pallas_call | solution.py:216
  349.5 5.5 %back.1 = (bf16[4,256,1536]{2,1,0:T(8,128)(2,1)}, bf16[4,256,1536]{2,1,0:T(8,128)(2,1)S(1)}, bf16[384,2048]{1,0:T(8,128)(2,1)S(1)}) custom-call(s32[1]{0:T(128)} %bitcast.pos_ref, f32[192,2048]{1,0:T(8,128)S(1)} %copy-done.10, f32[64,2048]{1,0:T(8,128)S(1)} %copy-done.20, f32[64,2048]{1,0:T(8,128)S(1)} %copy-done.21, f32[32,2048]{1,0:T(8,128)S(1)} %copy-done.15, ...), custom_call_target="tpu_custom_call" | custom-call | bytes 10000 | tf_op jit(solution)/shard_map/back/pallas_call | solution.py:742
  356.8 8.5 %pack.1 = bf16[1536,384]{1,0:T(8,128)(2,1)S(1)} custom-call(s32[1]{0:T(128)} %bitcast.pos_ref, bf16[384,2048]{1,0:T(8,128)(2,1)S(1)} %get-tuple-element.151.packed_ref, bf16[8,256,1536]{2,1,0:T(8,128)(2,1)} %bitcast.9.refs_10_.x_ref, f32[1,1536]{1,0:T(1,128)S(1)} %copy-done.29, bf16[1536,384]{1,0:T(8,128)(2,1)S(1)} %bitcast.61, f32[1536,128]{1,0:T(8,128)S(1)} %copy-done.39, ...), custom_call_target="tpu_custom_call" | custom-call | flops 49999998976 | bytes 10000 | tf_op jit(solution)/shard_map/pack/pallas_call | solution.py:805
  379.8 7.0 %out_grad.1 = f32[192,1536]{1,0:T(8,128)S(1)} custom-call(s32[1]{0:T(128)} %bitcast.pos_ref, bf16[192,2048]{1,0:T(8,128)(2,1)} %get-tuple-element.95.refs_0_, bf16[192,2048]{1,0:T(8,128)(2,1)S(1)} %copy-done.17, bf16[192,2048]{1,0:T(8,128)(2,1)S(1)} %copy-done.9, bf16[192,2048]{1,0:T(8,128)(2,1)} %collective-permute-done.11.refs_3_, ...), custom_call_target="tpu_custom_call" | custom-call | bytes 10000 | tf_op jit(solution)/shard_map/out_grad/pallas_call | solution.py:881
  390.8 11.0 %collective-permute-done.36.fd_ref = bf16[256,1536]{1,0:T(8,128)(2,1)S(1)} collective-permute-done((bf16[256,1536]{1,0:T(8,128)(2,1)S(1)}, bf16[256,1536]{1,0:T(8,128)(2,1)S(1)}, u32[]{:S(2)}, u32[]{:S(2)}) %collective-permute-start.36) | collective-permute-done | bytes 786464 | tf_op jit(solution)/shard_map/ppermute | solution.py:929
  402.2 16.8 %collective-permute-done.35.fy_ref = bf16[256,1536]{1,0:T(8,128)(2,1)S(1)} collective-permute-done((bf16[256,1536]{1,0:T(8,128)(2,1)S(1)}, bf16[256,1536]{1,0:T(8,128)(2,1)S(1)}, u32[]{:S(2)}, u32[]{:S(2)}) %collective-permute-start.35) | collective-permute-done | bytes 786464 | tf_op jit(solution)/shard_map/ppermute | solution.py:929
  433.2 5.4 %collective-permute-done.38 = bf16[48,1536]{1,0:T(8,128)(2,1)} collective-permute-done((bf16[48,1536]{1,0:T(8,128)(2,1)S(1)}, bf16[48,1536]{1,0:T(8,128)(2,1)}, u32[]{:S(2)}, u32[]{:S(2)}) %collective-permute-start.38) | collective-permute-done | bytes 147488 | tf_op jit(solution)/shard_map/ppermute | solution.py:966
  (252 shorter events, 126.6 us)
Async XLA Ops:
  7.2 124.7 %all-gather.3.cloned.1.call-start = ((), (), s32[]{:S(2)}) async-start(), calls=%async_computation.8 | async-start | bytes 4866048 | tf_op jit(solution)/shard_map/all_gather | solution.py:1021
  10.8 56.9 %all-to-all-start = ((bf16[32,48,384]{2,1,0:T(8,128)(2,1)}), bf16[32,48,384]{2,1,0:T(8,128)(2,1)S(1)}, u32[]{:S(2)}, u32[]{:S(2)}) async-start(bf16[32,48,384]{2,1,0:T(8,128)(2,1)} %send_weights.1), calls=%async_computation | async-start | bytes 2359296 | tf_op jit(solution)/shard_map/all_to_all | solution.py:971
  18.1 158.4 %all-gather.5.cloned.1.call-start = ((), (), s32[]{:S(2)}) async-start(), calls=%async_computation.9 | async-start | bytes 7077888 | tf_op jit(solution)/shard_map/all_gather | solution.py:1022
  21.5 47.4 %collective-permute-start = (bf16[256,1536]{1,0:T(8,128)(2,1)}, bf16[256,1536]{1,0:T(8,128)(2,1)}, u32[]{:S(2)}, u32[]{:S(2)}) collective-permute-start(bf16[256,1536]{1,0:T(8,128)(2,1)} %x_ref.1), channel_id=1, source_target_pairs={{0,1},{1,0},{2,3},{3,2},{4,5},{5,4},{6,7},{7,6},{8,9},{9,8},{10,11... | collective-permute-start | bytes 2359304 | tf_op jit(solution)/shard_map/ppermute | solution.py:929
  21.5 229.1 %reduce-scatter.5.cloned.1.call-start = ((), (), s32[]{:S(2)}) async-start(), calls=%async_computation.10 | async-start | bytes 1966080 | tf_op jit(solution)/shard_map/reduce_scatter | solution.py:1049
  76.5 39.9 %collective-permute-start.21 = (s32[8,256]{1,0:T(8,128)S(1)}, s32[8,256]{1,0:T(8,128)S(1)}, u32[]{:S(2)}, u32[]{:S(2)}) collective-permute-start(s32[8,256]{1,0:T(8,128)S(1)} %bitcast.78), channel_id=1, source_target_pairs={{0,6},{1,7},{2,4},{3,5},{4,2},{5,3},{6,0},{7,1},{8,14},{9,15},{10,... | collective-permute-start | bytes 24584 | tf_op jit(solution)/shard_map/ppermute | solution.py:929
  76.9 36.8 %collective-permute-start.17 = (s32[8,256]{1,0:T(8,128)S(1)}, s32[8,256]{1,0:T(8,128)S(1)}, u32[]{:S(2)}, u32[]{:S(2)}) collective-permute-start(s32[8,256]{1,0:T(8,128)S(1)} %bitcast.79), channel_id=1, source_target_pairs={{0,2},{1,3},{2,0},{3,1},{4,6},{5,7},{6,4},{7,5},{8,10},{9,11},{10,... | collective-permute-start | bytes 24584 | tf_op jit(solution)/shard_map/ppermute | solution.py:929
  116.3 36.3 %collective-permute-start.9 = (bf16[192,2048]{1,0:T(8,128)(2,1)}, bf16[192,2048]{1,0:T(8,128)(2,1)S(1)}, u32[]{:S(2)}, u32[]{:S(2)}) collective-permute-start(bf16[192,2048]{1,0:T(8,128)(2,1)} %get-tuple-element.95.refs_0_), channel_id=1, source_target_pairs={{0,1},{1,0},{2,3},{3,2},{4,5},{5,4},{6,7},{7,6},{8,9},{9,8},{10,11... | collective-permute-start | bytes 2359304 | tf_op jit(solution)/shard_map/ppermute | solution.py:929
  206.6 92.6 %reduce-scatter.11.cloned.1.call-start = ((), (), s32[]{:S(2)}) async-start(), calls=%async_computation.13 | async-start | bytes 1966080 | tf_op jit(solution)/shard_map/reduce_scatter | solution.py:1049
  243.7 40.7 %collective-permute-start.29 = (bf16[256,1536]{1,0:T(8,128)(2,1)}, bf16[256,1536]{1,0:T(8,128)(2,1)S(1)}, u32[]{:S(2)}, u32[]{:S(2)}) collective-permute-start(bf16[256,1536]{1,0:T(8,128)(2,1)} %get-tuple-element.220), channel_id=1, source_target_pairs={{0,6},{1,7},{2,4},{3,5},{4,2},{5,3},{6,0},{7,1},{8,14},{9,15},{10,... | collective-permute-start | bytes 2359304 | tf_op jit(solution)/shard_map/ppermute | solution.py:929
  243.8 40.6 %collective-permute-start.28 = (bf16[256,1536]{1,0:T(8,128)(2,1)}, bf16[256,1536]{1,0:T(8,128)(2,1)S(1)}, u32[]{:S(2)}, u32[]{:S(2)}) collective-permute-start(bf16[256,1536]{1,0:T(8,128)(2,1)} %get-tuple-element.221), channel_id=1, source_target_pairs={{0,4},{1,5},{2,6},{3,7},{4,0},{5,1},{6,2},{7,3},{8,12},{9,13},{10,... | collective-permute-start | bytes 2359304 | tf_op jit(solution)/shard_map/ppermute | solution.py:929
  245.5 38.9 %collective-permute-start.27 = (bf16[256,1536]{1,0:T(8,128)(2,1)}, bf16[256,1536]{1,0:T(8,128)(2,1)S(1)}, u32[]{:S(2)}, u32[]{:S(2)}) collective-permute-start(bf16[256,1536]{1,0:T(8,128)(2,1)} %get-tuple-element.222), channel_id=1, source_target_pairs={{0,2},{1,3},{2,0},{3,1},{4,6},{5,7},{6,4},{7,5},{8,10},{9,11},{10,... | collective-permute-start | bytes 2359304 | tf_op jit(solution)/shard_map/ppermute | solution.py:929
  247.2 36.3 %all-to-all-start.1 = ((f32[8,8,256]{2,1,0:T(8,128)}), f32[8,8,256]{2,1,0:T(8,128)S(1)}, u32[]{:S(2)}, u32[]{:S(2)}) async-start(f32[8,8,256]{2,1,0:T(8,128)} %get-tuple-element.137), calls=%async_computation.2 | async-start | bytes 131072 | tf_op jit(solution)/shard_map/all_to_all | solution.py:971
  250.6 173.9 %reduce-scatter.9.cloned.1.call-start = ((), (), s32[]{:S(2)}) async-start(), calls=%async_computation.12 | async-start | bytes 3932160 | tf_op jit(solution)/shard_map/reduce_scatter | solution.py:1050
  298.6 128.3 %reduce-scatter.7.cloned.1.call-start = ((), (), s32[]{:S(2)}) async-start(), calls=%async_computation.11 | async-start | bytes 3932160 | tf_op jit(solution)/shard_map/reduce_scatter | solution.py:1050
  305.5 69.8 %collective-permute-start.32 = (bf16[256,1536]{1,0:T(8,128)(2,1)}, bf16[256,1536]{1,0:T(8,128)(2,1)}, u32[]{:S(2)}, u32[]{:S(2)}) collective-permute-start(bf16[256,1536]{1,0:T(8,128)(2,1)} %get-tuple-element.217), channel_id=1, source_target_pairs={{0,6},{1,7},{2,4},{3,5},{4,2},{5,3},{6,0},{7,1},{8,14},{9,15},{10,... | collective-permute-start | bytes 2359304 | tf_op jit(solution)/shard_map/ppermute | solution.py:929
  308.4 67.3 %collective-permute-start.31 = (bf16[256,1536]{1,0:T(8,128)(2,1)}, bf16[256,1536]{1,0:T(8,128)(2,1)}, u32[]{:S(2)}, u32[]{:S(2)}) collective-permute-start(bf16[256,1536]{1,0:T(8,128)(2,1)} %get-tuple-element.218), channel_id=1, source_target_pairs={{0,4},{1,5},{2,6},{3,7},{4,0},{5,1},{6,2},{7,3},{8,12},{9,13},{10,... | collective-permute-start | bytes 2359304 | tf_op jit(solution)/shard_map/ppermute | solution.py:929
  309.0 66.8 %collective-permute-start.30 = (bf16[256,1536]{1,0:T(8,128)(2,1)}, bf16[256,1536]{1,0:T(8,128)(2,1)}, u32[]{:S(2)}, u32[]{:S(2)}) collective-permute-start(bf16[256,1536]{1,0:T(8,128)(2,1)} %get-tuple-element.219), channel_id=1, source_target_pairs={{0,2},{1,3},{2,0},{3,1},{4,6},{5,7},{6,4},{7,5},{8,10},{9,11},{10,... | collective-permute-start | bytes 2359304 | tf_op jit(solution)/shard_map/ppermute | solution.py:929
  366.3 65.1 %all-to-all-start.3 = ((bf16[32,48,384]{2,1,0:T(8,128)(2,1)}), bf16[32,48,384]{2,1,0:T(8,128)(2,1)S(1)}, u32[]{:S(2)}, u32[]{:S(2)}) async-start(bf16[32,48,384]{2,1,0:T(8,128)(2,1)} %bitcast.62), calls=%async_computation.4 | async-start | bytes 2359296 | tf_op jit(solution)/shard_map/all_to_all | solution.py:971
  374.7 44.3 %collective-permute-start.35 = (bf16[256,1536]{1,0:T(8,128)(2,1)S(1)}, bf16[256,1536]{1,0:T(8,128)(2,1)S(1)}, u32[]{:S(2)}, u32[]{:S(2)}) collective-permute-start(bf16[256,1536]{1,0:T(8,128)(2,1)S(1)} %get-tuple-element.215), channel_id=1, source_target_pairs={{0,4},{1,5},{2,6},{3,7},{4,0},{5,1},{6,2},{7,3},{8,12},{9,13},{10,... | collective-permute-start | bytes 2359304 | tf_op jit(solution)/shard_map/ppermute | solution.py:929
  375.3 45.4 %collective-permute-start.34 = (bf16[256,1536]{1,0:T(8,128)(2,1)S(1)}, bf16[256,1536]{1,0:T(8,128)(2,1)S(1)}, u32[]{:S(2)}, u32[]{:S(2)}) collective-permute-start(bf16[256,1536]{1,0:T(8,128)(2,1)S(1)} %get-tuple-element.216), channel_id=1, source_target_pairs={{0,2},{1,3},{2,0},{3,1},{4,6},{5,7},{6,4},{7,5},{8,10},{9,11},{10,... | collective-permute-start | bytes 2359304 | tf_op jit(solution)/shard_map/ppermute | solution.py:929
  387.0 46.2 %collective-permute-start.39 = (bf16[48,1536]{1,0:T(8,128)(2,1)S(1)}, bf16[48,1536]{1,0:T(8,128)(2,1)}, u32[]{:S(2)}, u32[]{:S(2)}) collective-permute-start(bf16[48,1536]{1,0:T(8,128)(2,1)S(1)} %get-tuple-element.223), channel_id=1, source_target_pairs={{0,24},{8,0},{16,8},{24,16},{1,25},{9,1},{17,9},{25,17},{2,26},{10... | collective-permute-start | bytes 442376 | tf_op jit(solution)/shard_map/ppermute | solution.py:966
  390.8 47.8 %collective-permute-start.38 = (bf16[48,1536]{1,0:T(8,128)(2,1)S(1)}, bf16[48,1536]{1,0:T(8,128)(2,1)}, u32[]{:S(2)}, u32[]{:S(2)}) collective-permute-start(bf16[48,1536]{1,0:T(8,128)(2,1)S(1)} %get-tuple-element.224), channel_id=1, source_target_pairs={{0,16},{8,24},{16,0},{24,8},{1,17},{9,25},{17,1},{25,9},{2,18},{10... | collective-permute-start | bytes 442376 | tf_op jit(solution)/shard_map/ppermute | solution.py:966
  401.8 36.8 %collective-permute-start.37 = (bf16[48,1536]{1,0:T(8,128)(2,1)S(1)}, bf16[48,1536]{1,0:T(8,128)(2,1)}, u32[]{:S(2)}, u32[]{:S(2)}) collective-permute-start(bf16[48,1536]{1,0:T(8,128)(2,1)S(1)} %get-tuple-element.225), channel_id=1, source_target_pairs={{0,8},{8,16},{16,24},{24,0},{1,9},{9,17},{17,25},{25,1},{2,10},{10... | collective-permute-start | bytes 442376 | tf_op jit(solution)/shard_map/ppermute | solution.py:966
  (77 other events, 988.2 us)
Sparse Core Ops, SparseCore 0:
  10.9 75.0 all-gather.2
  87.9 62.9 all-gather.4
  206.7 34.2 reduce-scatter.4
  243.2 34.2 reduce-scatter.10
  279.6 59.2 reduce-scatter.8
  341.0 85.8 reduce-scatter.6

commit v3 on v2

--- a/solution.py
+++ b/solution.py
@@ -508,10 +508,10 @@
         total = dot(dgu, up_ref[0], 1, 1)
         place = pos_ref[0] % 2 if h else 1 - pos_ref[0] % 2
         if e == 0:
-            sum_ref[rows] = total
+            sum_ref[rows] = total.astype(BF)
             dg_ref[place] = gate_grad
         else:
-            (keep_ref if h else give_ref)[0] = (sum_ref[rows] + total).astype(BF)
+            (keep_ref if h else give_ref)[0] = (sum_ref[rows].astype(F32) + total).astype(BF)
             dg_ref[place] = dg_in_ref[place] + gate_grad
     if e == 0:
         grad_acc[...] += dot(ag_ref[...], dy_ref[...], 0, 0)
@@ -530,7 +530,7 @@
     one = lambda a: pl.BlockSpec(
         (1,) + a.shape[1:], lambda s, pos: (e, 0, 0), pipeline_mode=pl.Buffered(1)
     )
-    sums = (spec((PAIR, D), row), shape((seq, D), F32))
+    sums = (spec((PAIR, D), row), shape((seq, D), BF))
     gate_grads = (spec((2, 8, BLK), blocks), shape((2 * half, 8, BLK), F32))
     outs = [
         (spec((PAIR, FF), row), shape((seq, FF), BF)),

time: 457 us -> 457 us (level)
  Pallas kernels: 203 us -> 194 us
  waiting for transfers between devices: 107 us -> 114 us
    ppermute x37, waiting for transfers between devices: 86 us -> 90.6 us  [swap(): return lax.ppermute(values, 'expert', [(i, i ^ bit) for i in range(count)])]
  transfers between devices with their start and end apart: 50 -> 50, of which waited for: 15 -> 14; matrix products, arithmetic and copies ran while one was open for 13% -> 13% of each run, Pallas kernels for 38% -> 36%
where the time goes in v3:
time: 457 us; the launch traced here: 449 us
  Pallas kernels  194 us (42%)
  waiting for transfers between devices  114 us (25%)
  starting transfers between devices  52.8 us (12%)
  local copies, waits for them, and re-layouts  46.5 us (10%)
  other arithmetic  26.4 us (6%)
  between operations  15.1 us (3%)
    ppermute x37, waiting for transfers between devices, swap(): return lax.ppermute(values, 'expert', [(i, i ^ bit) for i in range(count)])  90.6 us
    pallas_call x2, Pallas kernels, expert_pass(): call(functools.partial(expert_kernel, e), 'expert_%d' % e, (half,), [spec...  54.8 us
    unnamed x120, local copies, waits for them, and re-layouts  34 us
    ppermute x37, starting transfers between devices, swap(): return lax.ppermute(values, 'expert', [(i, i ^ bit) for i in range(count)])  26.5 us
    pallas_call x1, Pallas kernels, mix_forward(): call(functools.partial(mix_kernel, count), 'mix', (seq // PAIR,), [spec((...  22.2 us
    pallas_call x2, Pallas kernels, up_grad(): call(up_grad_kernel, 'up_grad', (D // rows,), [spec((seq, rows), lambda s...  21.8 us
    all_to_all x4, starting transfers between devices, exchange(): return lax.all_to_all(blocks, axes, split_axis=0, concat_axis=0, tiled=True)  21.8 us
    pallas_call x1, Pallas kernels, attn_backward(): pl.pallas_call(attn_bwd_kernel, grid_spec=pltpu.PrefetchScalarGridSpec(nu...  19.9 us
  transfers between devices with their start and end apart: 50, of which 14 were waited for; matrix products, arithmetic and copies ran while one was open for 13% of the time, Pallas kernels for 36%

profile of v3, /device:TPU:0, one launch (start us, length us, event | category | flops | bytes accessed | tf_op | source)
XLA Modules:
  0.0 448.8 jit_solution(854922241241663629)
XLA Ops:
  10.8 7.3 %all-to-all-start = ((bf16[32,48,384]{2,1,0:T(8,128)(2,1)}), bf16[32,48,384]{2,1,0:T(8,128)(2,1)S(1)}, u32[]{:S(2)}, u32[]{:S(2)}) async-start(bf16[32,48,384]{2,1,0:T(8,128)(2,1)} %send_weights.1), calls=%async_computation | async-start | bytes 2359296 | tf_op jit(solution)/shard_map/all_to_all | solution.py:971
  23.5 30.2 %collective-permute-done.3.refs_4_ = bf16[256,1536]{1,0:T(8,128)(2,1)S(1)} collective-permute-done((bf16[256,1536]{1,0:T(8,128)(2,1)}, bf16[256,1536]{1,0:T(8,128)(2,1)S(1)}, u32[]{:S(2)}, u32[]{:S(2)}) %collective-permute-start.3) | collective-permute-done | bytes 786464 | tf_op jit(solution)/shard_map/ppermute | solution.py:929
  58.0 6.6 %collective-permute-done.6.refs_7_ = bf16[128,1536]{1,0:T(8,128)(2,1)} collective-permute-done((bf16[128,1536]{1,0:T(8,128)(2,1)S(1)}, bf16[128,1536]{1,0:T(8,128)(2,1)}, u32[]{:S(2)}, u32[]{:S(2)}) %collective-permute-start.6) | collective-permute-done | bytes 393248 | tf_op jit(solution)/shard_map/ppermute | solution.py:929
  69.5 6.9 %qkv.1 = (bf16[192,2048]{1,0:T(8,128)(2,1)S(1)}, bf16[64,2048]{1,0:T(8,128)(2,1)S(1)}, bf16[64,2048]{1,0:T(8,128)(2,1)S(1)}, bf16[2048,64]{1,0:T(8,128)(2,1)S(1)}, bf16[2048,64]{1,0:T(8,128)(2,1)S(1)}) custom-call(s32[1]{0:T(128)} %bitcast.pos_ref, bf16[256,1536]{1,0:T(8,128)(2,1)} %x_ref.1, bf16[256,1536]{1,0:T(8,128)(2,1)} %collective-permute-done.refs_1_, ...), custom_call_target="tpu_custom_call" | custom-call | flops 399999991808 | bytes 10000 | tf_op jit(solution)/shard_map/qkv/pallas_call | solution.py:342
  79.5 13.7 %attn_fwd.1 = (bf16[192,2048]{1,0:T(8,128)(2,1)}, f32[192,2048]{1,0:T(8,128)S(1)}, f32[8,2048]{1,0:T(8,128)S(1)}) custom-call(s32[2,8]{1,0:T(2,128)S(1)} %pad_add_fusion.first_ref, bf16[192,2048]{1,0:T(8,128)(2,1)S(1)} %get-tuple-element.92.q_ref, bf16[2048,64]{1,0:T(8,128)(2,1)S(1)} %get-tuple-element.93.k_ref, ...), custom_call_target="tpu_custom_call" | custom-call | flops 49999998976 | bytes 10000 | tf_op jit(solution)/shard_map/attn_fwd/pallas_call | solution.py:183
  113.9 11.4 %collective-permute-done.19 = s32[8,256]{1,0:T(8,128)S(1)} collective-permute-done((s32[8,256]{1,0:T(8,128)S(1)}, s32[8,256]{1,0:T(8,128)S(1)}, u32[]{:S(2)}, u32[]{:S(2)}) %collective-permute-start.19) | collective-permute-done | bytes 8224 | tf_op jit(solution)/shard_map/ppermute | solution.py:929
  131.8 6.6 %copy.35 = bf16[1536,1536]{0,1:T(8,128)(2,1)} copy(bf16[1536,1536]{1,0:T(8,128)(2,1)} %all-gather.3.cloned.1.call-done) | data formatting | bytes 9437184 | tf_op jit(solution)/shard_map/all_gather | solution.py:1021
  138.4 9.1 %collective-permute-done.15.refs_7_ = bf16[96,2048]{1,0:T(8,128)(2,1)S(1)} collective-permute-done((bf16[96,2048]{1,0:T(8,128)(2,1)}, bf16[96,2048]{1,0:T(8,128)(2,1)S(1)}, u32[]{:S(2)}, u32[]{:S(2)}) %collective-permute-start.15) | collective-permute-done | bytes 393248 | tf_op jit(solution)/shard_map/ppermute | solution.py:929
  154.2 22.2 %mix.1 = (bf16[2048,1536]{1,0:T(8,128)(2,1)}, f32[2048,128]{1,0:T(8,128)}, f32[256,1536]{1,0:T(8,128)}, bf16[256,1536]{1,0:T(8,128)(2,1)}, f32[256,128]{1,0:T(8,128)}) custom-call(s32[1]{0:T(128)} %bitcast.pos_ref, bf16[192,2048]{1,0:T(8,128)(2,1)} %get-tuple-element.95.refs_0_, bf16[192,2048]{1,0:T(8,128)(2,1)} %copy-done.16, bf16[192,2048]{1,0:T(8,128)(2,1)} %copy-done.8, ...), custom_call_target="tpu_custom_call" | custom-call | flops 49999998976 | bytes 10000 | tf_op jit(solution)/shard_map/mix/pallas_call | solution.py:448
  176.5 29.7 %expert_0.1 = (bf16[2048,512]{1,0:T(8,128)(2,1)}, bf16[2048,1024]{1,0:T(8,128)(2,1)}, bf16[2048,1536]{1,0:T(8,128)(2,1)}, f32[8,8,256]{2,1,0:T(8,128)}, bf16[4,512,384]{2,1,0:T(8,128)(2,1)}) custom-call(s32[1]{0:T(128)} %bitcast.pos_ref, bf16[2048,1536]{1,0:T(8,128)(2,1)} %get-tuple-element.125.h2_ref, ...), custom_call_target="tpu_custom_call" | custom-call | flops 5000000000 | bytes 10000 | tf_op jit(solution)/shard_map/expert_0/pallas_call | solution.py:544
  206.3 25.1 %expert_1.1 = (bf16[2048,512]{1,0:T(8,128)(2,1)}, bf16[2048,1024]{1,0:T(8,128)(2,1)}, bf16[4,256,1536]{2,1,0:T(8,128)(2,1)}, bf16[4,256,1536]{2,1,0:T(8,128)(2,1)}, f32[8,8,256]{2,1,0:T(8,128)}) custom-call(s32[1]{0:T(128)} %bitcast.pos_ref, bf16[2048,1536]{1,0:T(8,128)(2,1)} %get-tuple-element.125.h2_ref, ...), custom_call_target="tpu_custom_call" | custom-call | flops 5000000000 | bytes 10000 | tf_op jit(solution)/shard_map/expert_1/pallas_call | solution.py:544
  231.4 7.3 %down_grad.1 = bf16[4,512,384]{2,1,0:T(8,128)(2,1)} custom-call(s32[1]{0:T(128)} %bitcast.pos_ref, bf16[2048,512]{1,0:T(8,128)(2,1)} %get-tuple-element.128.ag_ref.refs_1_, bf16[2048,1536]{1,0:T(8,128)(2,1)} %all-gather.5.cloned.1.call-done.dy_ref), custom_call_target="tpu_custom_call" | custom-call | bytes 10000 | tf_op jit(solution)/shard_map/down_grad/pallas_call | solution.py:580
  249.2 10.9 %up_grad.2 = bf16[1536,1024]{1,0:T(8,128)(2,1)} custom-call(s32[1]{0:T(128)} %bitcast.pos_ref, bf16[2048,1536]{1,0:T(8,128)(2,1)} %get-tuple-element.125.h2_ref, bf16[2048,1024]{1,0:T(8,128)(2,1)} %get-tuple-element.124.dgu_ref), custom_call_target="tpu_custom_call" | custom-call | bytes 10000 | tf_op jit(solution)/shard_map/up_grad/pallas_call | solution.py:599
  260.1 10.9 %up_grad.3 = bf16[1536,1024]{1,0:T(8,128)(2,1)} custom-call(s32[1]{0:T(128)} %bitcast.pos_ref, bf16[2048,1536]{1,0:T(8,128)(2,1)} %get-tuple-element.125.h2_ref, bf16[2048,1024]{1,0:T(8,128)(2,1)} %get-tuple-element.126.dgu_ref), custom_call_target="tpu_custom_call" | custom-call | bytes 10000 | tf_op jit(solution)/shard_map/up_grad/pallas_call | solution.py:599
  271.1 10.6 %combine.1 = (bf16[4,256,1536]{2,1,0:T(8,128)(2,1)}, bf16[4,256,1536]{2,1,0:T(8,128)(2,1)}) custom-call(s32[1]{0:T(128)} %bitcast.pos_ref, bf16[2048,512]{1,0:T(8,128)(2,1)} %get-tuple-element.127.refs_0_, bf16[2048,512]{1,0:T(8,128)(2,1)} %get-tuple-element.128.ag_ref.refs_1_, bf16[2,512,1536]{2,1,0:T(8,128)(2,1)} %refs_2_.1), custom_call_target="tpu_custom_call" | custom-call | bytes 10000 | tf_op jit(solution)/shard_map/combine/pallas_call | solution.py:624
  284.3 9.3 %middle.1 = (f32[256,1536]{1,0:T(8,128)}, bf16[256,1536]{1,0:T(8,128)(2,1)}, bf16[8,384,256]{2,1,0:T(8,128)(2,1)}, f32[1536,128]{1,0:T(8,128)}, f32[8,1536]{1,0:T(8,128)}) custom-call(s32[1]{0:T(128)} %bitcast.pos_ref, bf16[4,256,1536]{2,1,0:T(8,128)(2,1)} %get-tuple-element.133.keep_ref, bf16[4,256,1536]{2,1,0:T(8,128)(2,1)} %collective-permute-done.25.got_ref, ...), custom_call_target="tpu_custom_call" | custom-call | flops 99999997952 | bytes 10000 | tf_op jit(solution)/shard_map/middle/pallas_call | solution.py:684
  308.1 11.2 %all-to-all-done.2.da_ref.refs_10_ = bf16[8,384,256]{2,1,0:T(8,128)(2,1)S(1)} async-done(((bf16[8,384,256]{2,1,0:T(8,128)(2,1)}), bf16[8,384,256]{2,1,0:T(8,128)(2,1)S(1)}, u32[]{:S(2)}, u32[]{:S(2)}) %all-to-all-start.2) | async-done | bytes 1572896 | tf_op jit(solution)/shard_map/all_to_all | solution.py:971
  320.5 19.9 %attn_bwd.1 = (f32[192,2048]{1,0:T(8,128)}, f32[64,2048]{1,0:T(8,128)}, f32[64,2048]{1,0:T(8,128)}) custom-call(s32[2,8]{1,0:T(2,128)} %copy-done.30, bf16[192,2048]{1,0:T(8,128)(2,1)} %copy-done.34, bf16[8,384,256]{2,1,0:T(8,128)(2,1)} %copy-done.2, f32[192,2048]{1,0:T(8,128)} %copy-done.33, f32[8,2048]{1,0:T(8,128)} %copy-done.40, ...), custom_call_target="tpu_custom_call" | custom-call | flops 20000000000 | bytes 10000 | tf_op jit(solution)/shard_map/attn_bwd/pallas_call | solution.py:216
  351.1 8.6 %pack.1 = bf16[1536,384]{1,0:T(8,128)(2,1)S(1)} custom-call(s32[1]{0:T(128)} %bitcast.pos_ref, bf16[384,2048]{1,0:T(8,128)(2,1)S(1)} %get-tuple-element.151.packed_ref, bf16[8,256,1536]{2,1,0:T(8,128)(2,1)} %bitcast.9.refs_10_.x_ref, f32[1,1536]{1,0:T(1,128)S(1)} %copy-done.29, bf16[1536,384]{1,0:T(8,128)(2,1)S(1)} %bitcast.61, f32[1536,128]{1,0:T(8,128)S(1)} %copy-done.39, ...), custom_call_target="tpu_custom_call" | custom-call | flops 49999998976 | bytes 10000 | tf_op jit(solution)/shard_map/pack/pallas_call | solution.py:805
  360.7 7.0 %all-to-all-start.3 = ((bf16[32,48,384]{2,1,0:T(8,128)(2,1)}), bf16[32,48,384]{2,1,0:T(8,128)(2,1)S(1)}, u32[]{:S(2)}, u32[]{:S(2)}) async-start(bf16[32,48,384]{2,1,0:T(8,128)(2,1)} %bitcast.62), calls=%async_computation.4 | async-start | bytes 2359296 | tf_op jit(solution)/shard_map/all_to_all | solution.py:971
  378.4 7.0 %out_grad.1 = f32[192,1536]{1,0:T(8,128)S(1)} custom-call(s32[1]{0:T(128)} %bitcast.pos_ref, bf16[192,2048]{1,0:T(8,128)(2,1)} %get-tuple-element.95.refs_0_, bf16[192,2048]{1,0:T(8,128)(2,1)S(1)} %copy-done.17, bf16[192,2048]{1,0:T(8,128)(2,1)S(1)} %copy-done.9, bf16[192,2048]{1,0:T(8,128)(2,1)} %collective-permute-done.11.refs_3_, ...), custom_call_target="tpu_custom_call" | custom-call | bytes 10000 | tf_op jit(solution)/shard_map/out_grad/pallas_call | solution.py:881
  389.4 11.2 %collective-permute-done.36.fd_ref = bf16[256,1536]{1,0:T(8,128)(2,1)S(1)} collective-permute-done((bf16[256,1536]{1,0:T(8,128)(2,1)S(1)}, bf16[256,1536]{1,0:T(8,128)(2,1)S(1)}, u32[]{:S(2)}, u32[]{:S(2)}) %collective-permute-start.36) | collective-permute-done | bytes 786464 | tf_op jit(solution)/shard_map/ppermute | solution.py:929
  400.9 16.5 %collective-permute-done.35.fy_ref = bf16[256,1536]{1,0:T(8,128)(2,1)S(1)} collective-permute-done((bf16[256,1536]{1,0:T(8,128)(2,1)S(1)}, bf16[256,1536]{1,0:T(8,128)(2,1)S(1)}, u32[]{:S(2)}, u32[]{:S(2)}) %collective-permute-start.35) | collective-permute-done | bytes 786464 | tf_op jit(solution)/shard_map/ppermute | solution.py:929
  423.1 6.5 %reduce-scatter.7.cloned.1.call-done = bf16[384,1024]{1,0:T(8,128)(2,1)} async-done(((bf16[1536,1024]{1,0:T(8,128)(2,1)}), bf16[384,1024]{1,0:T(8,128)(2,1)}) %reduce-scatter.7.cloned.1.call-update) | async-done | bytes 786448 | tf_op jit(solution)/shard_map/reduce_scatter | solution.py:1050
  (252 shorter events, 128.1 us)
Async XLA Ops:
  7.2 124.6 %all-gather.3.cloned.1.call-start = ((), (), s32[]{:S(2)}) async-start(), calls=%async_computation.8 | async-start | bytes 4866048 | tf_op jit(solution)/shard_map/all_gather | solution.py:1021
  10.8 56.9 %all-to-all-start = ((bf16[32,48,384]{2,1,0:T(8,128)(2,1)}), bf16[32,48,384]{2,1,0:T(8,128)(2,1)S(1)}, u32[]{:S(2)}, u32[]{:S(2)}) async-start(bf16[32,48,384]{2,1,0:T(8,128)(2,1)} %send_weights.1), calls=%async_computation | async-start | bytes 2359296 | tf_op jit(solution)/shard_map/all_to_all | solution.py:971
  18.1 158.4 %all-gather.5.cloned.1.call-start = ((), (), s32[]{:S(2)}) async-start(), calls=%async_computation.9 | async-start | bytes 7077888 | tf_op jit(solution)/shard_map/all_gather | solution.py:1022
  20.0 35.7 %collective-permute-start.1 = (bf16[256,1536]{1,0:T(8,128)(2,1)}, bf16[256,1536]{1,0:T(8,128)(2,1)S(1)}, u32[]{:S(2)}, u32[]{:S(2)}) collective-permute-start(bf16[256,1536]{1,0:T(8,128)(2,1)} %x_ref.1), channel_id=1, source_target_pairs={{0,2},{1,3},{2,0},{3,1},{4,6},{5,7},{6,4},{7,5},{8,10},{9,11},{10,... | collective-permute-start | bytes 2359304 | tf_op jit(solution)/shard_map/ppermute | solution.py:929
  21.5 47.4 %collective-permute-start = (bf16[256,1536]{1,0:T(8,128)(2,1)}, bf16[256,1536]{1,0:T(8,128)(2,1)}, u32[]{:S(2)}, u32[]{:S(2)}) collective-permute-start(bf16[256,1536]{1,0:T(8,128)(2,1)} %x_ref.1), channel_id=1, source_target_pairs={{0,1},{1,0},{2,3},{3,2},{4,5},{5,4},{6,7},{7,6},{8,9},{9,8},{10,11... | collective-permute-start | bytes 2359304 | tf_op jit(solution)/shard_map/ppermute | solution.py:929
  21.5 227.7 %reduce-scatter.5.cloned.1.call-start = ((), (), s32[]{:S(2)}) async-start(), calls=%async_computation.10 | async-start | bytes 1966080 | tf_op jit(solution)/shard_map/reduce_scatter | solution.py:1049
  76.5 36.9 %collective-permute-start.21 = (s32[8,256]{1,0:T(8,128)S(1)}, s32[8,256]{1,0:T(8,128)S(1)}, u32[]{:S(2)}, u32[]{:S(2)}) collective-permute-start(s32[8,256]{1,0:T(8,128)S(1)} %bitcast.78), channel_id=1, source_target_pairs={{0,6},{1,7},{2,4},{3,5},{4,2},{5,3},{6,0},{7,1},{8,14},{9,15},{10,... | collective-permute-start | bytes 24584 | tf_op jit(solution)/shard_map/ppermute | solution.py:929
  113.4 39.2 %collective-permute-start.9 = (bf16[192,2048]{1,0:T(8,128)(2,1)}, bf16[192,2048]{1,0:T(8,128)(2,1)S(1)}, u32[]{:S(2)}, u32[]{:S(2)}) collective-permute-start(bf16[192,2048]{1,0:T(8,128)(2,1)} %get-tuple-element.95.refs_0_), channel_id=1, source_target_pairs={{0,1},{1,0},{2,3},{3,2},{4,5},{5,4},{6,7},{7,6},{8,9},{9,8},{10,11... | collective-permute-start | bytes 2359304 | tf_op jit(solution)/shard_map/ppermute | solution.py:929
  206.2 92.1 %reduce-scatter.11.cloned.1.call-start = ((), (), s32[]{:S(2)}) async-start(), calls=%async_computation.13 | async-start | bytes 1966080 | tf_op jit(solution)/shard_map/reduce_scatter | solution.py:1049
  242.1 40.8 %collective-permute-start.29 = (bf16[256,1536]{1,0:T(8,128)(2,1)}, bf16[256,1536]{1,0:T(8,128)(2,1)S(1)}, u32[]{:S(2)}, u32[]{:S(2)}) collective-permute-start(bf16[256,1536]{1,0:T(8,128)(2,1)} %get-tuple-element.220), channel_id=1, source_target_pairs={{0,6},{1,7},{2,4},{3,5},{4,2},{5,3},{6,0},{7,1},{8,14},{9,15},{10,... | collective-permute-start | bytes 2359304 | tf_op jit(solution)/shard_map/ppermute | solution.py:929
  242.9 40.0 %collective-permute-start.28 = (bf16[256,1536]{1,0:T(8,128)(2,1)}, bf16[256,1536]{1,0:T(8,128)(2,1)S(1)}, u32[]{:S(2)}, u32[]{:S(2)}) collective-permute-start(bf16[256,1536]{1,0:T(8,128)(2,1)} %get-tuple-element.221), channel_id=1, source_target_pairs={{0,4},{1,5},{2,6},{3,7},{4,0},{5,1},{6,2},{7,3},{8,12},{9,13},{10,... | collective-permute-start | bytes 2359304 | tf_op jit(solution)/shard_map/ppermute | solution.py:929
  244.2 38.7 %collective-permute-start.27 = (bf16[256,1536]{1,0:T(8,128)(2,1)}, bf16[256,1536]{1,0:T(8,128)(2,1)S(1)}, u32[]{:S(2)}, u32[]{:S(2)}) collective-permute-start(bf16[256,1536]{1,0:T(8,128)(2,1)} %get-tuple-element.222), channel_id=1, source_target_pairs={{0,2},{1,3},{2,0},{3,1},{4,6},{5,7},{6,4},{7,5},{8,10},{9,11},{10,... | collective-permute-start | bytes 2359304 | tf_op jit(solution)/shard_map/ppermute | solution.py:929
  245.6 36.4 %all-to-all-start.1 = ((f32[8,8,256]{2,1,0:T(8,128)}), f32[8,8,256]{2,1,0:T(8,128)S(1)}, u32[]{:S(2)}, u32[]{:S(2)}) async-start(f32[8,8,256]{2,1,0:T(8,128)} %get-tuple-element.137), calls=%async_computation.2 | async-start | bytes 131072 | tf_op jit(solution)/shard_map/all_to_all | solution.py:971
  249.0 174.1 %reduce-scatter.9.cloned.1.call-start = ((), (), s32[]{:S(2)}) async-start(), calls=%async_computation.12 | async-start | bytes 3932160 | tf_op jit(solution)/shard_map/reduce_scatter | solution.py:1050
  297.7 131.9 %reduce-scatter.7.cloned.1.call-start = ((), (), s32[]{:S(2)}) async-start(), calls=%async_computation.11 | async-start | bytes 3932160 | tf_op jit(solution)/shard_map/reduce_scatter | solution.py:1050
  304.6 69.4 %collective-permute-start.32 = (bf16[256,1536]{1,0:T(8,128)(2,1)}, bf16[256,1536]{1,0:T(8,128)(2,1)}, u32[]{:S(2)}, u32[]{:S(2)}) collective-permute-start(bf16[256,1536]{1,0:T(8,128)(2,1)} %get-tuple-element.217), channel_id=1, source_target_pairs={{0,6},{1,7},{2,4},{3,5},{4,2},{5,3},{6,0},{7,1},{8,14},{9,15},{10,... | collective-permute-start | bytes 2359304 | tf_op jit(solution)/shard_map/ppermute | solution.py:929
  307.5 67.0 %collective-permute-start.31 = (bf16[256,1536]{1,0:T(8,128)(2,1)}, bf16[256,1536]{1,0:T(8,128)(2,1)}, u32[]{:S(2)}, u32[]{:S(2)}) collective-permute-start(bf16[256,1536]{1,0:T(8,128)(2,1)} %get-tuple-element.218), channel_id=1, source_target_pairs={{0,4},{1,5},{2,6},{3,7},{4,0},{5,1},{6,2},{7,3},{8,12},{9,13},{10,... | collective-permute-start | bytes 2359304 | tf_op jit(solution)/shard_map/ppermute | solution.py:929
  308.1 66.4 %collective-permute-start.30 = (bf16[256,1536]{1,0:T(8,128)(2,1)}, bf16[256,1536]{1,0:T(8,128)(2,1)}, u32[]{:S(2)}, u32[]{:S(2)}) collective-permute-start(bf16[256,1536]{1,0:T(8,128)(2,1)} %get-tuple-element.219), channel_id=1, source_target_pairs={{0,2},{1,3},{2,0},{3,1},{4,6},{5,7},{6,4},{7,5},{8,10},{9,11},{10,... | collective-permute-start | bytes 2359304 | tf_op jit(solution)/shard_map/ppermute | solution.py:929
  360.7 72.1 %all-to-all-start.3 = ((bf16[32,48,384]{2,1,0:T(8,128)(2,1)}), bf16[32,48,384]{2,1,0:T(8,128)(2,1)S(1)}, u32[]{:S(2)}, u32[]{:S(2)}) async-start(bf16[32,48,384]{2,1,0:T(8,128)(2,1)} %bitcast.62), calls=%async_computation.4 | async-start | bytes 2359296 | tf_op jit(solution)/shard_map/all_to_all | solution.py:971
  373.5 43.9 %collective-permute-start.35 = (bf16[256,1536]{1,0:T(8,128)(2,1)S(1)}, bf16[256,1536]{1,0:T(8,128)(2,1)S(1)}, u32[]{:S(2)}, u32[]{:S(2)}) collective-permute-start(bf16[256,1536]{1,0:T(8,128)(2,1)S(1)} %get-tuple-element.215), channel_id=1, source_target_pairs={{0,4},{1,5},{2,6},{3,7},{4,0},{5,1},{6,2},{7,3},{8,12},{9,13},{10,... | collective-permute-start | bytes 2359304 | tf_op jit(solution)/shard_map/ppermute | solution.py:929
  374.1 45.3 %collective-permute-start.34 = (bf16[256,1536]{1,0:T(8,128)(2,1)S(1)}, bf16[256,1536]{1,0:T(8,128)(2,1)S(1)}, u32[]{:S(2)}, u32[]{:S(2)}) collective-permute-start(bf16[256,1536]{1,0:T(8,128)(2,1)S(1)} %get-tuple-element.216), channel_id=1, source_target_pairs={{0,2},{1,3},{2,0},{3,1},{4,6},{5,7},{6,4},{7,5},{8,10},{9,11},{10,... | collective-permute-start | bytes 2359304 | tf_op jit(solution)/shard_map/ppermute | solution.py:929
  385.6 49.0 %collective-permute-start.39 = (bf16[48,1536]{1,0:T(8,128)(2,1)S(1)}, bf16[48,1536]{1,0:T(8,128)(2,1)}, u32[]{:S(2)}, u32[]{:S(2)}) collective-permute-start(bf16[48,1536]{1,0:T(8,128)(2,1)S(1)} %get-tuple-element.223), channel_id=1, source_target_pairs={{0,24},{8,0},{16,8},{24,16},{1,25},{9,1},{17,9},{25,17},{2,26},{10... | collective-permute-start | bytes 442376 | tf_op jit(solution)/shard_map/ppermute | solution.py:966
  389.4 49.9 %collective-permute-start.38 = (bf16[48,1536]{1,0:T(8,128)(2,1)S(1)}, bf16[48,1536]{1,0:T(8,128)(2,1)}, u32[]{:S(2)}, u32[]{:S(2)}) collective-permute-start(bf16[48,1536]{1,0:T(8,128)(2,1)S(1)} %get-tuple-element.224), channel_id=1, source_target_pairs={{0,16},{8,24},{16,0},{24,8},{1,17},{9,25},{17,1},{25,9},{2,18},{10... | collective-permute-start | bytes 442376 | tf_op jit(solution)/shard_map/ppermute | solution.py:966
  400.6 38.7 %collective-permute-start.37 = (bf16[48,1536]{1,0:T(8,128)(2,1)S(1)}, bf16[48,1536]{1,0:T(8,128)(2,1)}, u32[]{:S(2)}, u32[]{:S(2)}) collective-permute-start(bf16[48,1536]{1,0:T(8,128)(2,1)S(1)} %get-tuple-element.225), channel_id=1, source_target_pairs={{0,8},{8,16},{16,24},{24,0},{1,9},{9,17},{17,25},{25,1},{2,10},{10... | collective-permute-start | bytes 442376 | tf_op jit(solution)/shard_map/ppermute | solution.py:966
  (77 other events, 962.3 us)
Sparse Core Ops, SparseCore 0:
  10.9 75.0 all-gather.2
  87.9 62.9 all-gather.4
  206.3 35.3 reduce-scatter.4
  243.9 34.2 reduce-scatter.10
  280.3 59.2 reduce-scatter.8
  341.7 87.7 reduce-scatter.6
